TPU v7x, 128 devices: a whole 4x4x4 slice. The times are simulated.
128 devices in a mesh: dom: 32 (over z, x, core), bin: 4 (over y).
Axes of the slice: x: 4, y: 4, z: 4, core: 2. Of those that a mesh axis runs over, the one named last changes fastest.
Arguments:
- displacement: float32 [3, 256, 64, 512], P(None, 'dom', 'bin'), may hold values from -0.3 to 0.3
- velocity: float32 [3, 256, 64, 512], P(None, 'dom', 'bin'), may hold values from -0.3 to 0.3
- moduli: float32 [2, 256, 64, 512], P(None, 'dom', 'bin'), may hold values from 0.2 to 2
- nodal_mass: float32 [256, 64, 512], P('dom', 'bin'), may hold values from 0.5 to 2
- segment_node: int32 [131072], P(('dom', 'bin')), may hold values from 0 to 65535
- segment_base: float32 [3, 131072], P(None, ('dom', 'bin')), may hold values from 0 to 1
- contact_bin: int32 [4, 1024, 1], P(None, ('dom', 'bin')), may hold values from 0 to 3; in each aligned block of 8 rows (0 to 7, 8 to 15, ..., all dimensions but the last counted through in order) at most 4 rows name the same one
- element_tile: int32 [256, 64, 512], P('dom', 'bin'), may hold values from 0 to 32767, as said below
Outputs:
- new_displacement: float32 [3, 256, 64, 512], P(None, 'dom', 'bin')
- new_velocity: float32 [3, 256, 64, 512], P(None, 'dom', 'bin')
- tile_heat: float32 [32768], P(('dom', 'bin'))
Inputs may be any that keep to these rules, and one draw needn't show every extreme that they name: `contact_bin`: in each substep no device sends more than 4 of its blocks to one bin, and at least one device sends exactly 4. `segment_node`: A node of the holding device's own block, numbered row-major over (8, 16, 512). `element_tile`: tiles are numbered device-major (256 to a device, devices in the order dom, then bin). An element's tile belongs to the device that holds it, except that elements of a device's first or last layer along the first dimension may take a tile of the device one step lower or higher along dom (same bin index).
All inputs are finite; a program needn't handle non-finite values.
Results may differ from a plain program's by a relative error of at most 0.0003.
Values sent between devices are 32-bit elements; how exact they have to be, the bound alone decides.
A program may use at most 128 MiB of HBM per device.

v0:
```python
import jax
import jax.numpy as jnp
from jax import lax
from jax.sharding import PartitionSpec as P

SUB = 4
SEG = 128
TILE_DEV = 256


RADIUS = 0.09
PENALTY = 4.0
SHORT_GAIN = 100.0
TIME_STEP = 0.2
CORNERS = ((0, 0, 0), (0, 0, 1), (0, 1, 0), (0, 1, 1), (1, 0, 0), (1, 0, 1), (1, 1, 0), (1, 1, 1))


def shifted(value, axis, steps):
    count = lax.axis_size(axis)
    first, last = (max(0, -steps), min(count, count - steps))
    return lax.ppermute(value, axis, [(source, source + steps) for source in range(first, last)])


def corner_forces(padded, moduli_used, extent_x, extent_y):
    pieces = []
    for a, b, c in CORNERS:
        piece = padded[:, a : a + extent_x, b : b + extent_y]
        if c == 1:
            piece = jnp.roll(piece, -1, axis=3)
        pieces.append(piece)
    corner_signs = [[2 * bit - 1 for bit in corner] for corner in CORNERS]
    gradient = [
        [0.25 * sum((corner_signs[k][q] * pieces[k][p] for k in range(8))) for q in range(3)]
        for p in range(3)
    ]
    volume_strain = gradient[0][0] + gradient[1][1] + gradient[2][2]
    stress = [
        [
            moduli_used[1] * (gradient[p][q] + gradient[q][p])
            + (moduli_used[0] * volume_strain if p == q else 0.0)
            for q in range(3)
        ]
        for p in range(3)
    ]
    corner_list = []
    for k in range(8):
        corner_list.append(
            jnp.stack(
                [
                    -0.25 * sum((corner_signs[k][q] * stress[p][q] for q in range(3)))
                    for p in range(3)
                ]
            )
        )
    return corner_list


def spread_corners(corner_list):
    nodal = 0.0
    for k in range(8):
        a, b, c = CORNERS[k]
        moved = jnp.roll(corner_list[k], c, axis=3)
        nodal = nodal + jnp.pad(moved, ((0, 0), (a, 1 - a), (b, 1 - b), (0, 0)))
    return nodal


def contact_terms(segment_pool, alive_mask):
    row_blocks = segment_pool.reshape(3, -1, SEG).transpose(1, 0, 2)

    def one_block(target):
        offsets = target[:, :, None] - segment_pool[:, None, :]
        distance = jnp.sqrt(jnp.sum(offsets * offsets, axis=0))
        pressure = jnp.maximum(RADIUS - distance, 0.0) * alive_mask[None, :]
        pushing = PENALTY * jnp.sum(
            offsets * (pressure / jnp.maximum(distance, 0.25 * RADIUS))[None], axis=2
        )
        heating = SHORT_GAIN * jnp.sum(pressure * pressure, axis=1)
        return (pushing, heating)

    return lax.map(one_block, row_blocks)


def relay_each(partial_heat):
    from_upper = shifted(partial_heat[0], "dom", -1)
    from_lower = shifted(partial_heat[2], "dom", 1)
    return partial_heat[1] + from_upper + from_lower


def per_device(
    displacement,
    velocity,
    moduli,
    nodal_mass,
    segment_node,
    segment_base,
    contact_bin,
    element_tile,
):
    size_x = displacement.shape[1]
    size_y = displacement.shape[2]
    block_count = segment_node.shape[0] // SEG
    bin_count = lax.axis_size("bin")
    capacity = block_count // 2
    own_device = lax.axis_index("dom") * bin_count + lax.axis_index("bin")
    segment_tile = element_tile.reshape(-1)[segment_node]
    tile_offset = segment_tile // TILE_DEV - own_device
    tile_side = tile_offset // bin_count + 1
    tile_slot = tile_side * TILE_DEV + segment_tile % TILE_DEV
    slot_numbers = jnp.arange(bin_count * capacity, dtype=jnp.int32)
    bin_numbers = jnp.arange(bin_count, dtype=jnp.int32)
    tile_heat = jnp.zeros((TILE_DEV,), jnp.float32)
    for step in range(SUB):
        points = segment_base + displacement.reshape(3, -1)[:, segment_node]
        target_bin = contact_bin[step, :, 0]
        onehot = (target_bin[:, None] == bin_numbers[None, :]).astype(jnp.int32)
        slot_rank = jnp.cumsum(onehot, axis=0) - onehot
        slot_index = target_bin * capacity + jnp.sum(slot_rank * onehot, axis=1)
        placing = (slot_index[:, None] == slot_numbers[None, :]).astype(jnp.float32)
        blocks = (
            points.reshape(3, block_count, SEG).transpose(1, 0, 2).reshape(block_count, 3 * SEG)
        )
        outgoing = jnp.dot(placing.T, blocks, precision=lax.Precision.HIGHEST).reshape(
            bin_count, capacity, 3, SEG
        )
        filled = jnp.sum(placing, axis=0).reshape(bin_count, capacity)
        incoming, arrived = (
            lax.all_to_all(outgoing, "bin", split_axis=0, concat_axis=0, tiled=True),
            lax.all_to_all(filled, "bin", split_axis=0, concat_axis=0, tiled=True),
        )
        segment_pool = incoming.transpose(2, 0, 1, 3).reshape(3, -1)
        alive_mask = jnp.repeat(arrived.reshape(-1), SEG)
        pushing, heating = contact_terms(segment_pool, alive_mask)
        results = jnp.concatenate([pushing, heating[:, None, :]], axis=1).reshape(
            bin_count, capacity, 4, SEG
        )
        returned = lax.all_to_all(results, "bin", split_axis=0, concat_axis=0, tiled=True)
        per_block = jnp.dot(
            placing,
            returned.reshape(bin_count * capacity, 4 * SEG),
            precision=lax.Precision.HIGHEST,
        ).reshape(block_count, 4, SEG)
        segment_push = per_block[:, :3].transpose(1, 0, 2).reshape(3, -1)
        segment_heat = per_block[:, 3].reshape(-1)
        partial_heat = jax.ops.segment_sum(
            segment_heat, tile_slot, num_segments=3 * TILE_DEV
        ).reshape(3, TILE_DEV)
        tile_heat = tile_heat + relay_each(partial_heat)
        contact = (
            jnp.zeros((3, displacement[0].size), jnp.float32)
            .at[:, segment_node]
            .add(segment_push)
            .reshape(displacement.shape)
        )
        column = shifted(displacement[:, :, :1], "bin", -1)
        widened = jnp.concatenate([displacement, column], axis=2)
        layer = shifted(widened[:, :1], "dom", -1)
        padded = jnp.concatenate([widened, layer], axis=1)
        nodal = spread_corners(corner_forces(padded, moduli, size_x, size_y))
        lower_layer = shifted(nodal[:, size_x:], "dom", 1)
        nodal = nodal[:, :size_x] + jnp.pad(lower_layer, ((0, 0), (0, size_x - 1), (0, 0), (0, 0)))
        lower_column = shifted(nodal[:, :, size_y:], "bin", 1)
        internal = nodal[:, :, :size_y] + jnp.pad(
            lower_column, ((0, 0), (0, 0), (0, size_y - 1), (0, 0))
        )
        velocity = velocity + TIME_STEP * (internal + contact) / nodal_mass[None]
        displacement = displacement + TIME_STEP * velocity
    return (displacement, velocity, tile_heat)


def solution(mesh):
    placed = (
        P(None, "dom", "bin", None),
        P(None, "dom", "bin", None),
        P(None, "dom", "bin", None),
        P("dom", "bin", None),
        P(("dom", "bin")),
        P(None, ("dom", "bin")),
        P(None, ("dom", "bin"), None),
        P("dom", "bin", None),
    )
    return jax.shard_map(
        per_device,
        mesh=mesh,
        in_specs=placed,
        out_specs=(P(None, "dom", "bin", None), P(None, "dom", "bin", None), P(("dom", "bin"))),
        check_vma=False,
    )
```

profile of v0, /device:TPU:39, one launch (start us, length us, event | category | flops | bytes accessed | tf_op | source)
XLA Modules:
  0.0 668.0 jit_solution(15218174932830043144)
XLA Ops:
  3.6 4.2 all-to-all-start.1
  10.1 17.4 %copy.119 = f32[3,8,16,512]{0,3,2,1:T(8,128)} copy(f32[3,8,16,512]{3,2,1,0:T(8,128)} %param.16) | data formatting | bytes 1572864 | tf_op args[0]
  27.8 13.4 %gather_fusion = f32[1024,3]{1,0:T(8,128)S(1)} fusion(f32[3,65536]{0,1:T(8,128)} %bitcast.309, s32[1024]{0:T(1024)S(1)} %get-tuple-element.589), kind=kCustom, calls=%fused_computation | custom fusion | bytes 28672 | tf_op jit(solution)/shard_map/gather | solution.py:113
  42.1 6.2 gather_fusion.4
  49.7 9.0 %all_to_all.76 = f32[4,1,4]{2,1,0:T(1,128)S(1)} all-to-all(f32[4,1,4]{2,1,0:T(1,128)S(1)} %bitcast.359), channel_id=1, replica_groups=mesh['dom'=32,'bin'=4] {'bin'}, dimensions={0} | all-to-all | bytes 128 | tf_op jit(solution)/shard_map/all_to_all | solution.py:128
  58.8 6.4 all_to_all.77
  65.2 6.4 all_to_all.78
  81.4 26.4 %while.52 = (s32[]{:T(128)}, f32[16,3,128]{2,1,0:T(4,128)S(1)}, f32[16,128]{1,0:T(8,128)S(1)}, f32[16,3,128]{2,0,1:T(8,128)S(1)}, f32[3,4,4,128]{3,2,1,0:T(4,128)S(1)}, /*index=5*/f32[16]{0:T(128)S(1)}, s32[]{:T(128)}, s32[]{:T(128)}) while((s32[]{:T(128)}, f32[16,3,128]{2,1,0:T(4,128)S(1)}, f32[16,128]{1,0:T(8,128)S(1)}, ...), condition=%wide.region_7.8_spmd.clone, body=%wide.region_3.7_spmd.clone.sunk | while | flops 6291458 | bytes 4326569 | solution.py:80
  108.5 7.2 %collective-permute-start.1 = (f32[3,1,17,512]{3,2,1,0:T(8,128)S(1)}, f32[3,1,17,512]{3,2,1,0:T(8,128)S(1)}, u32[]{:S(2)}, u32[]{:S(2)}) collective-permute-start(f32[3,1,17,512]{3,2,1,0:T(8,128)S(1)} %slice.1195), channel_id=1, source_target_pairs={{4,0},{8,4},{12,8},{16,12},{20,16},{24,20},{28,24},{32,28},{36,32}... | collective-permute-start | bytes 313352 | tf_op jit(solution)/shard_map/ppermute | solution.py:21
  116.3 4.5 all-to-all-start.2
  125.4 5.0 fusion.58
  137.3 3.9 collective-permute-start.3
  141.4 19.2 %scatter_custom_fusion = f32[3,65536]{0,1:T(8,128)} fusion(s32[1024]{0:T(1024)S(1)} %get-tuple-element.590, f32[1024,3]{1,0:T(8,128)S(1)} %bitcast.330, f32[]{:T(128)} %constant.149.clone.1), kind=kCustom, calls=%fused_computation.71 | custom fusion | flops 3072 | bytes 786436 | tf_op jit(solution)/shard_map/scatter-add | solution.py:151
  160.6 20.3 %copy.129 = f32[3,8,16,512]{3,2,1,0:T(8,128)} copy(f32[3,8,16,512]{0,3,2,1:T(8,128)} %bitcast.305) | data formatting | bytes 1572864 | tf_op jit(solution)/shard_map/reshape | solution.py:152
  183.8 16.4 %copy.130 = f32[3,8,16,512]{0,3,2,1:T(8,128)} copy(f32[3,8,16,512]{3,2,1,0:T(8,128)S(1)} %get-tuple-element.404) | data formatting | bytes 1572864 | tf_op jit(solution)/shard_map/add | solution.py:166
  200.2 13.4 %gather_fusion.1 = f32[1024,3]{1,0:T(8,128)S(1)} fusion(f32[3,65536]{0,1:T(8,128)} %bitcast.311, s32[1024]{0:T(1024)S(1)} %get-tuple-element.589), kind=kCustom, calls=%fused_computation.1 | custom fusion | bytes 28672 | tf_op jit(solution)/shard_map/gather | solution.py:113
  214.7 3.7 all-to-all-start.3
  218.3 7.7 %scatter_custom_fusion.4 = f32[768]{0:T(1024)S(1)} fusion(s32[1024]{0:T(1024)} %bitcast.362, f32[1024]{0:T(1024)S(1)} %slice_bitcast_fusion.7, f32[]{:T(128)} %constant.149.clone.1), kind=kCustom, calls=%fused_computation.735 | custom fusion | flops 1024 | bytes 3584 | tf_op jit(solution)/shard_map/scatter-add | solution.py:144
  226.1 26.4 %while.53 = (s32[]{:T(128)}, f32[16,3,128]{2,1,0:T(4,128)S(1)}, f32[16,128]{1,0:T(8,128)S(1)}, f32[16,3,128]{2,0,1:T(8,128)S(1)}, f32[3,4,4,128]{3,2,1,0:T(4,128)S(1)}, /*index=5*/f32[16]{0:T(128)S(1)}, s32[]{:T(128)}, s32[]{:T(128)}) while((s32[]{:T(128)}, f32[16,3,128]{2,1,0:T(4,128)S(1)}, f32[16,128]{1,0:T(8,128)S(1)}, ...), condition=%wide.region_16.17_spmd.clone, body=%wide.region_12.16_spmd.clone.sunk | while | flops 6291458 | bytes 4326569 | solution.py:80
  253.2 4.2 all-to-all-start.5
  257.4 7.6 %collective-permute-start.17 = (f32[256]{0:T(256)S(1)}, f32[256]{0:T(256)S(1)}, u32[]{:S(2)}, u32[]{:S(2)}) collective-permute-start(f32[256]{0:T(256)S(1)} %get-tuple-element.582), channel_id=1, source_target_pairs={{0,4},{4,8},{8,12},{12,16},{16,20},{20,24},{24,28},{28,32},{32,36}... | collective-permute-start | bytes 3080 | tf_op jit(solution)/shard_map/ppermute | solution.py:21
  275.1 6.5 collective-permute-done.5
  285.4 5.0 fusion.47
  299.5 19.5 %scatter_custom_fusion.1 = f32[3,65536]{0,1:T(8,128)} fusion(s32[1024]{0:T(1024)} %copy-done.19, f32[1024,3]{1,0:T(8,128)S(1)} %bitcast.331, f32[]{:T(128)} %constant.149.clone.1), kind=kCustom, calls=%fused_computation.69 | custom fusion | flops 3072 | bytes 786944 | tf_op jit(solution)/shard_map/scatter-add | solution.py:151
  319.0 20.3 %copy.140 = f32[3,8,16,512]{3,2,1,0:T(8,128)} copy(f32[3,8,16,512]{0,3,2,1:T(8,128)} %bitcast.306) | data formatting | bytes 1572864 | tf_op jit(solution)/shard_map/reshape | solution.py:152
  339.2 7.7 %scatter_custom_fusion.5 = f32[768]{0:T(1024)S(1)} fusion(s32[1024]{0:T(1024)} %bitcast.363, f32[1024]{0:T(1024)S(1)} %slice_bitcast_fusion.6, f32[]{:T(128)} %constant.149.clone.1), kind=kCustom, calls=%fused_computation.733 | custom fusion | flops 1024 | bytes 3584 | tf_op jit(solution)/shard_map/scatter-add | solution.py:144
  349.9 16.4 %copy.141 = f32[3,8,16,512]{0,3,2,1:T(8,128)} copy(f32[3,8,16,512]{3,2,1,0:T(8,128)S(1)} %get-tuple-element.385) | data formatting | bytes 1572864 | tf_op jit(solution)/shard_map/add | solution.py:166
  366.4 13.4 %gather_fusion.2 = f32[1024,3]{1,0:T(8,128)S(1)} fusion(f32[3,65536]{0,1:T(8,128)} %bitcast.312, s32[1024]{0:T(1024)S(1)} %copy-done.14), kind=kCustom, calls=%fused_computation.2 | custom fusion | bytes 28672 | tf_op jit(solution)/shard_map/gather | solution.py:113
  384.1 6.8 %collective-permute-start.19 = (f32[256]{0:T(256)S(1)}, f32[256]{0:T(256)S(1)}, u32[]{:S(2)}, u32[]{:S(2)}) collective-permute-start(f32[256]{0:T(256)S(1)} %get-tuple-element.584), channel_id=1, source_target_pairs={{0,4},{4,8},{8,12},{12,16},{16,20},{20,24},{24,28},{28,32},{32,36}... | collective-permute-start | bytes 3080 | tf_op jit(solution)/shard_map/ppermute | solution.py:21
  394.2 26.4 %while.54 = (s32[]{:T(128)}, f32[16,3,128]{2,1,0:T(4,128)S(1)}, f32[16,128]{1,0:T(8,128)S(1)}, f32[16,3,128]{2,0,1:T(8,128)S(1)}, f32[3,4,4,128]{3,2,1,0:T(4,128)S(1)}, /*index=5*/f32[16]{0:T(128)S(1)}, s32[]{:T(128)}, s32[]{:T(128)}) while((s32[]{:T(128)}, f32[16,3,128]{2,1,0:T(4,128)S(1)}, f32[16,128]{1,0:T(8,128)S(1)}, ...), condition=%wide.region_25.26_spmd.clone, body=%wide.region_21.25_spmd.clone.sunk | while | flops 6291458 | bytes 4326569 | solution.py:80
  421.2 5.4 all-to-all-start.8
  429.2 6.5 collective-permute-done.9
  439.6 5.0 fusion.36
  452.2 3.9 collective-permute-start.11
  456.3 19.3 %scatter_custom_fusion.2 = f32[3,65536]{0,1:T(8,128)} fusion(s32[1024]{0:T(1024)} %copy-done.19, f32[1024,3]{1,0:T(8,128)S(1)} %bitcast.332, f32[]{:T(128)} %constant.149.clone.1), kind=kCustom, calls=%fused_computation.67 | custom fusion | flops 3072 | bytes 786944 | tf_op jit(solution)/shard_map/scatter-add | solution.py:151
  475.6 20.3 %copy.151 = f32[3,8,16,512]{3,2,1,0:T(8,128)} copy(f32[3,8,16,512]{0,3,2,1:T(8,128)} %bitcast.307) | data formatting | bytes 1572864 | tf_op jit(solution)/shard_map/reshape | solution.py:152
  498.8 16.4 %copy.152 = f32[3,8,16,512]{0,3,2,1:T(8,128)} copy(f32[3,8,16,512]{3,2,1,0:T(8,128)S(1)} %get-tuple-element.366) | data formatting | bytes 1572864 | tf_op jit(solution)/shard_map/add | solution.py:166
  515.2 14.6 %gather_fusion.3 = f32[1024,3]{1,0:T(8,128)} fusion(f32[3,65536]{0,1:T(8,128)} %bitcast.310, s32[1024]{0:T(1024)S(1)} %copy-done.14), kind=kCustom, calls=%fused_computation.3 | custom fusion | bytes 28672 | tf_op jit(solution)/shard_map/gather | solution.py:113
  531.9 3.7 all-to-all-start.9
  535.5 7.7 %scatter_custom_fusion.6 = f32[768]{0:T(1024)S(1)} fusion(s32[1024]{0:T(1024)} %bitcast.364, f32[1024]{0:T(1024)S(1)} %slice_bitcast_fusion.5, f32[]{:T(128)} %constant.149.clone.1), kind=kCustom, calls=%fused_computation.731 | custom fusion | flops 1024 | bytes 3584 | tf_op jit(solution)/shard_map/scatter-add | solution.py:144
  543.4 26.4 %while.55 = (s32[]{:T(128)}, f32[16,3,128]{2,1,0:T(4,128)S(1)}, f32[16,128]{1,0:T(8,128)S(1)}, f32[16,3,128]{2,0,1:T(8,128)S(1)}, f32[3,4,4,128]{3,2,1,0:T(4,128)S(1)}, /*index=5*/f32[16]{0:T(128)S(1)}, s32[]{:T(128)}, s32[]{:T(128)}) while((s32[]{:T(128)}, f32[16,3,128]{2,1,0:T(4,128)S(1)}, f32[16,128]{1,0:T(8,128)S(1)}, ...), condition=%wide.region_34.35_spmd.clone, body=%wide.region_30.34_spmd.clone.sunk | while | flops 6291458 | bytes 4326569 | solution.py:80
  570.4 4.2 all-to-all-start.11
  579.1 7.8 %scatter_custom_fusion.7 = f32[768]{0:T(1024)S(1)} fusion(s32[1024]{0:T(1024)} %bitcast.365, f32[1024]{0:T(1024)S(1)} %slice_bitcast_fusion.4, f32[]{:T(128)} %constant.149.clone.1), kind=kCustom, calls=%fused_computation.729 | custom fusion | flops 1024 | bytes 3584 | tf_op jit(solution)/shard_map/scatter-add | solution.py:144
  591.1 7.3 %collective-permute-done.13 = f32[3,1,17,512]{3,2,1,0:T(8,128)S(1)} collective-permute-done((f32[3,1,17,512]{3,2,1,0:T(8,128)S(1)}, f32[3,1,17,512]{3,2,1,0:T(8,128)S(1)}, u32[]{:S(2)}, u32[]{:S(2)}) %collective-permute-start.13) | collective-permute-done | bytes 104480 | tf_op jit(solution)/shard_map/ppermute | solution.py:21
  602.3 4.9 fusion.25
  609.5 19.6 %scatter_custom_fusion.3 = f32[3,65536]{0,1:T(8,128)} fusion(s32[1024]{0:T(1024)} %copy-done.19, f32[1024,3]{1,0:T(8,128)S(1)} %bitcast.329, f32[]{:T(128)} %constant.149.clone.1), kind=kCustom, calls=%fused_computation.65 | custom fusion | flops 3072 | bytes 786944 | tf_op jit(solution)/shard_map/scatter-add | solution.py:151
  629.1 19.5 %copy.162 = f32[3,8,16,512]{3,2,1,0:T(8,128)S(1)} copy(f32[3,8,16,512]{0,3,2,1:T(8,128)} %bitcast.304) | data formatting | bytes 1572864 | tf_op jit(solution)/shard_map/reshape | solution.py:152
  653.1 5.3 collective-permute-start.23
  (890 shorter events, 219.8 us)
Async XLA Ops:
  2.8 38.6 %copy-start.26 = (s32[8]{0:T(128)}, s32[8]{0:T(128)S(1)}, u32[]{:S(2)}) copy-start(s32[8]{0:T(128)S(1)} %get-tuple-element.593) | copy-start | bytes 100
  2.9 38.8 %copy-start.24 = (s32[8]{0:T(128)}, s32[8]{0:T(128)S(1)}, u32[]{:S(2)}) copy-start(s32[8]{0:T(128)S(1)} %get-tuple-element.592) | copy-start | bytes 100
  2.9 38.9 %copy-start.22 = (s32[8]{0:T(128)}, s32[8]{0:T(128)S(1)}, u32[]{:S(2)}) copy-start(s32[8]{0:T(128)S(1)} %get-tuple-element.591) | copy-start | bytes 100
  3.6 46.1 %all-to-all-start.1 = ((f32[4,1,4]{2,1,0:T(1,128)}), f32[4,1,4]{2,1,0:T(1,128)S(1)}, u32[]{:S(2)}, u32[]{:S(2)}) async-start(f32[4,1,4]{2,1,0:T(1,128)} %bitcast.15), calls=%async_computation.1 | async-start | bytes 4096 | tf_op jit(solution)/shard_map/all_to_all | solution.py:128
  8.8 18.7 %copy-start.18 = (s32[1024]{0:T(1024)S(1)}, s32[1024]{0:T(1024)}, u32[]{:S(2)}) copy-start(s32[1024]{0:T(1024)} %param.20) | copy-start | bytes 12292
  8.8 18.7 %copy-start.17 = (f32[3,1024]{1,0:T(4,128)S(1)}, f32[3,1024]{1,0:T(4,128)}, u32[]{:S(2)}) copy-start(f32[3,1024]{1,0:T(4,128)} %param.21) | copy-start | bytes 36868
  8.8 98.9 %collective-permute-start = (f32[3,8,1,512]{3,2,1,0:T(1,128)S(1)}, f32[3,8,1,512]{3,2,1,0:T(1,128)S(1)}, u32[]{:S(2)}, u32[]{:S(2)}) collective-permute-start(f32[3,8,1,512]{3,2,1,0:T(1,128)S(1)} %slice.973), channel_id=1, source_target_pairs={{1,0},{2,1},{3,2},{5,4},{6,5},{7,6},{9,8},{10,9},{11,10},{13,12},{... | collective-permute-start | bytes 147464 | tf_op jit(solution)/shard_map/ppermute | solution.py:21
  27.6 20.7 %copy-start.20 = (s32[4,4]{1,0:T(4,128)}, s32[4,4]{1,0:T(4,128)S(1)}, u32[]{:S(2)}) copy-start(s32[4,4]{1,0:T(4,128)S(1)} %multiply_add_fusion.64) | copy-start | bytes 196
  27.6 113.8 %copy-start.19 = (s32[1024]{0:T(1024)}, s32[1024]{0:T(1024)S(1)}, u32[]{:S(2)}) copy-start(s32[1024]{0:T(1024)S(1)} %get-tuple-element.590) | copy-start | bytes 12292
  27.6 172.6 %copy-start.13 = (s32[1024]{0:T(1024)}, s32[1024]{0:T(1024)S(1)}, u32[]{:S(2)}) copy-start(s32[1024]{0:T(1024)S(1)} %get-tuple-element.589) | copy-start | bytes 12292
  42.1 32.8 %copy-start.1 = (f32[3,8,16,512]{3,2,1,0:T(8,128)S(1)}, f32[3,8,16,512]{3,2,1,0:T(8,128)}, u32[]{:S(2)}) copy-start(f32[3,8,16,512]{3,2,1,0:T(8,128)} %param.16) | copy-start | bytes 2359300
  71.6 9.7 %all-to-all-start = ((f32[4,4,3,128]{3,1,2,0:T(4,128)}), f32[4,4,3,128]{3,1,2,0:T(4,128)S(1)}, u32[]{:S(2)}, u32[]{:S(2)}) async-start(f32[4,4,3,128]{3,1,2,0:T(4,128)} %fusion.162), calls=%async_computation | async-start | bytes 49152 | tf_op jit(solution)/shard_map/all_to_all | solution.py:127
  108.5 12.3 %collective-permute-start.1 = (f32[3,1,17,512]{3,2,1,0:T(8,128)S(1)}, f32[3,1,17,512]{3,2,1,0:T(8,128)S(1)}, u32[]{:S(2)}, u32[]{:S(2)}) collective-permute-start(f32[3,1,17,512]{3,2,1,0:T(8,128)S(1)} %slice.1195), channel_id=1, source_target_pairs={{4,0},{8,4},{12,8},{16,12},{20,16},{24,20},{28,24},{32,28},{36,32}... | collective-permute-start | bytes 313352 | tf_op jit(solution)/shard_map/ppermute | solution.py:21
  116.3 17.7 %all-to-all-start.2 = ((f32[4,4,4,128]{3,2,1,0:T(4,128)}), f32[4,4,4,128]{3,2,1,0:T(4,128)S(1)}, u32[]{:S(2)}, u32[]{:S(2)}) async-start(f32[4,4,4,128]{3,2,1,0:T(4,128)} %pad_maximum_fusion.23), calls=%async_computation.2 | async-start | bytes 65536 | tf_op jit(solution)/shard_map/all_to_all | solution.py:136
  130.4 5.7 collective-permute-start.2
  137.3 43.6 %collective-permute-start.3 = (f32[3,8,1,512]{3,2,1,0:T(1,128)S(1)}, f32[3,8,1,512]{3,2,1,0:T(1,128)S(1)}, u32[]{:S(2)}, u32[]{:S(2)}) collective-permute-start(f32[3,8,1,512]{3,2,1,0:T(1,128)S(1)} %slice.1231), channel_id=1, source_target_pairs={{0,1},{1,2},{2,3},{4,5},{5,6},{6,7},{8,9},{9,10},{10,11},{12,13},{... | collective-permute-start | bytes 147464 | tf_op jit(solution)/shard_map/ppermute | solution.py:21
  160.6 20.3 %copy-start.4 = (f32[8,16,512]{2,1,0:T(8,128)S(1)}, f32[8,16,512]{2,1,0:T(8,128)}, u32[]{:S(2)}) copy-start(f32[8,16,512]{2,1,0:T(8,128)} %param.19) | copy-start | bytes 786436
  214.7 11.4 %all-to-all-start.3 = ((f32[4,4,3,128]{3,1,2,0:T(4,128)}), f32[4,4,3,128]{3,1,2,0:T(4,128)S(1)}, u32[]{:S(2)}, u32[]{:S(2)}) async-start(f32[4,4,3,128]{3,1,2,0:T(4,128)} %fusion.160), calls=%async_computation.3 | async-start | bytes 49152 | tf_op jit(solution)/shard_map/all_to_all | solution.py:127
  253.2 15.1 %all-to-all-start.5 = ((f32[4,4,4,128]{3,2,1,0:T(4,128)}), f32[4,4,4,128]{3,2,1,0:T(4,128)S(1)}, u32[]{:S(2)}, u32[]{:S(2)}) async-start(f32[4,4,4,128]{3,2,1,0:T(4,128)} %pad_maximum_fusion.24), calls=%async_computation.5 | async-start | bytes 65536 | tf_op jit(solution)/shard_map/all_to_all | solution.py:136
  257.4 391.2 %collective-permute-start.17 = (f32[256]{0:T(256)S(1)}, f32[256]{0:T(256)S(1)}, u32[]{:S(2)}, u32[]{:S(2)}) collective-permute-start(f32[256]{0:T(256)S(1)} %get-tuple-element.582), channel_id=1, source_target_pairs={{0,4},{4,8},{8,12},{12,16},{16,20},{20,24},{24,28},{28,32},{32,36}... | collective-permute-start | bytes 3080 | tf_op jit(solution)/shard_map/ppermute | solution.py:21
  265.0 385.6 %collective-permute-start.16 = (f32[256]{0:T(256)S(1)}, f32[256]{0:T(256)S(1)}, u32[]{:S(2)}, u32[]{:S(2)}) collective-permute-start(f32[256]{0:T(256)S(1)} %get-tuple-element.581), channel_id=1, source_target_pairs={{4,0},{8,4},{12,8},{16,12},{20,16},{24,20},{28,24},{32,28},{36,32}... | collective-permute-start | bytes 3080 | tf_op jit(solution)/shard_map/ppermute | solution.py:21
  267.0 5.1 collective-permute-start.4
  272.1 9.4 %collective-permute-start.5 = (f32[3,1,17,512]{3,2,1,0:T(8,128)S(1)}, f32[3,1,17,512]{3,2,1,0:T(8,128)S(1)}, u32[]{:S(2)}, u32[]{:S(2)}) collective-permute-start(f32[3,1,17,512]{3,2,1,0:T(8,128)S(1)} %fusion.143), channel_id=1, source_target_pairs={{4,0},{8,4},{12,8},{16,12},{20,16},{24,20},{28,24},{32,28},{36,32}... | collective-permute-start | bytes 313352 | tf_op jit(solution)/shard_map/ppermute | solution.py:21
  290.4 4.0 collective-permute-start.6
  295.6 51.4 %collective-permute-start.7 = (f32[3,8,1,512]{3,2,1,0:T(1,128)S(1)}, f32[3,8,1,512]{3,2,1,0:T(1,128)S(1)}, u32[]{:S(2)}, u32[]{:S(2)}) collective-permute-start(f32[3,8,1,512]{3,2,1,0:T(1,128)S(1)} %slice.1278), channel_id=1, source_target_pairs={{0,1},{1,2},{2,3},{4,5},{5,6},{6,7},{8,9},{9,10},{10,11},{12,13},{... | collective-permute-start | bytes 147464 | tf_op jit(solution)/shard_map/ppermute | solution.py:21
  319.0 28.0 %copy-start.5 = (f32[8,16,512]{2,1,0:T(8,128)S(1)}, f32[8,16,512]{2,1,0:T(8,128)}, u32[]{:S(2)}) copy-start(f32[8,16,512]{2,1,0:T(8,128)} %param.19) | copy-start | bytes 786436
  366.4 27.8 %copy-start.16 = (f32[16]{0:T(128)S(1)}, f32[16]{0:T(128)}, u32[]{:S(2)}) copy-start(f32[16]{0:T(128)} %reshape.590) | copy-start | bytes 196
  380.8 13.3 %all-to-all-start.6 = ((f32[4,4,3,128]{3,1,2,0:T(4,128)}), f32[4,4,3,128]{3,1,2,0:T(4,128)S(1)}, u32[]{:S(2)}, u32[]{:S(2)}) async-start(f32[4,4,3,128]{3,1,2,0:T(4,128)} %fusion.158), calls=%async_computation.6 | async-start | bytes 49152 | tf_op jit(solution)/shard_map/all_to_all | solution.py:127
  384.1 269.0 %collective-permute-start.19 = (f32[256]{0:T(256)S(1)}, f32[256]{0:T(256)S(1)}, u32[]{:S(2)}, u32[]{:S(2)}) collective-permute-start(f32[256]{0:T(256)S(1)} %get-tuple-element.584), channel_id=1, source_target_pairs={{0,4},{4,8},{8,12},{12,16},{16,20},{20,24},{24,28},{28,32},{32,36}... | collective-permute-start | bytes 3080 | tf_op jit(solution)/shard_map/ppermute | solution.py:21
  390.9 269.6 %collective-permute-start.18 = (f32[256]{0:T(256)S(1)}, f32[256]{0:T(256)S(1)}, u32[]{:S(2)}, u32[]{:S(2)}) collective-permute-start(f32[256]{0:T(256)S(1)} %get-tuple-element.583), channel_id=1, source_target_pairs={{4,0},{8,4},{12,8},{16,12},{20,16},{24,20},{28,24},{32,28},{36,32}... | collective-permute-start | bytes 3080 | tf_op jit(solution)/shard_map/ppermute | solution.py:21
  392.8 33.7 %collective-permute-start.8 = (f32[3,8,1,512]{3,2,1,0:T(1,128)S(1)}, f32[3,8,1,512]{3,2,1,0:T(1,128)S(1)}, u32[]{:S(2)}, u32[]{:S(2)}) collective-permute-start(f32[3,8,1,512]{3,2,1,0:T(1,128)S(1)} %slice.1285), channel_id=1, source_target_pairs={{1,0},{2,1},{3,2},{5,4},{6,5},{7,6},{9,8},{10,9},{11,10},{13,12},{... | collective-permute-start | bytes 147464 | tf_op jit(solution)/shard_map/ppermute | solution.py:21
  421.2 26.4 %all-to-all-start.8 = ((f32[4,4,4,128]{3,2,1,0:T(4,128)}), f32[4,4,4,128]{3,2,1,0:T(4,128)S(1)}, u32[]{:S(2)}, u32[]{:S(2)}) async-start(f32[4,4,4,128]{3,2,1,0:T(4,128)} %pad_maximum_fusion.25), calls=%async_computation.8 | async-start | bytes 65536 | tf_op jit(solution)/shard_map/all_to_all | solution.py:136
  426.6 9.1 %collective-permute-start.9 = (f32[3,1,17,512]{3,2,1,0:T(8,128)S(1)}, f32[3,1,17,512]{3,2,1,0:T(8,128)S(1)}, u32[]{:S(2)}, u32[]{:S(2)}) collective-permute-start(f32[3,1,17,512]{3,2,1,0:T(8,128)S(1)} %fusion.142), channel_id=1, source_target_pairs={{4,0},{8,4},{12,8},{16,12},{20,16},{24,20},{28,24},{32,28},{36,32}... | collective-permute-start | bytes 313352 | tf_op jit(solution)/shard_map/ppermute | solution.py:21
  445.7 4.0 collective-permute-start.10
  452.2 43.7 %collective-permute-start.11 = (f32[3,8,1,512]{3,2,1,0:T(1,128)S(1)}, f32[3,8,1,512]{3,2,1,0:T(1,128)S(1)}, u32[]{:S(2)}, u32[]{:S(2)}) collective-permute-start(f32[3,8,1,512]{3,2,1,0:T(1,128)S(1)} %slice.1325), channel_id=1, source_target_pairs={{0,1},{1,2},{2,3},{4,5},{5,6},{6,7},{8,9},{9,10},{10,11},{12,13},{... | collective-permute-start | bytes 147464 | tf_op jit(solution)/shard_map/ppermute | solution.py:21
  475.6 20.3 %copy-start.6 = (f32[8,16,512]{2,1,0:T(8,128)S(1)}, f32[8,16,512]{2,1,0:T(8,128)}, u32[]{:S(2)}) copy-start(f32[8,16,512]{2,1,0:T(8,128)} %param.19) | copy-start | bytes 786436
  515.2 28.2 %copy-start.15 = (f32[16]{0:T(128)S(1)}, f32[16]{0:T(128)}, u32[]{:S(2)}) copy-start(f32[16]{0:T(128)} %reshape.597) | copy-start | bytes 196
  531.9 11.4 %all-to-all-start.9 = ((f32[4,4,3,128]{3,1,2,0:T(4,128)}), f32[4,4,3,128]{3,1,2,0:T(4,128)S(1)}, u32[]{:S(2)}, u32[]{:S(2)}) async-start(f32[4,4,3,128]{3,1,2,0:T(4,128)} %fusion.156), calls=%async_computation.9 | async-start | bytes 49152 | tf_op jit(solution)/shard_map/all_to_all | solution.py:127
  570.4 8.5 %all-to-all-start.11 = ((f32[4,4,4,128]{3,2,1,0:T(4,128)}), f32[4,4,4,128]{3,2,1,0:T(4,128)S(1)}, u32[]{:S(2)}, u32[]{:S(2)}) async-start(f32[4,4,4,128]{3,2,1,0:T(4,128)} %pad_maximum_fusion.26), calls=%async_computation.11 | async-start | bytes 65536 | tf_op jit(solution)/shard_map/all_to_all | solution.py:136
  574.6 12.2 %collective-permute-start.12 = (f32[3,8,1,512]{3,2,1,0:T(1,128)S(1)}, f32[3,8,1,512]{3,2,1,0:T(1,128)S(1)}, u32[]{:S(2)}, u32[]{:S(2)}) collective-permute-start(f32[3,8,1,512]{3,2,1,0:T(1,128)S(1)} %slice.1332), channel_id=1, source_target_pairs={{1,0},{2,1},{3,2},{5,4},{6,5},{7,6},{9,8},{10,9},{11,10},{13,12},{... | collective-permute-start | bytes 147464 | tf_op jit(solution)/shard_map/ppermute | solution.py:21
  586.9 11.6 %collective-permute-start.13 = (f32[3,1,17,512]{3,2,1,0:T(8,128)S(1)}, f32[3,1,17,512]{3,2,1,0:T(8,128)S(1)}, u32[]{:S(2)}, u32[]{:S(2)}) collective-permute-start(f32[3,1,17,512]{3,2,1,0:T(8,128)S(1)} %fusion.141), channel_id=1, source_target_pairs={{4,0},{8,4},{12,8},{16,12},{20,16},{24,20},{28,24},{32,28},{36,32}... | collective-permute-start | bytes 313352 | tf_op jit(solution)/shard_map/ppermute | solution.py:21
  607.3 51.1 %collective-permute-start.14 = (f32[3,1,17,512]{3,2,1,0:T(8,128)S(1)}, f32[3,1,17,512]{3,2,1,0:T(8,128)S(1)}, u32[]{:S(2)}, u32[]{:S(2)}) collective-permute-start(f32[3,1,17,512]{3,2,1,0:T(8,128)S(1)} %slice.1370), channel_id=1, source_target_pairs={{0,4},{4,8},{8,12},{12,16},{16,20},{20,24},{24,28},{28,32},{32,36}... | collective-permute-start | bytes 313352 | tf_op jit(solution)/shard_map/ppermute | solution.py:21
  648.6 17.4 %copy-start.10 = (f32[3,8,16,512]{3,2,1,0:T(8,128)S(1)}, f32[3,8,16,512]{3,2,1,0:T(8,128)}, u32[]{:S(2)}) copy-start(f32[3,8,16,512]{3,2,1,0:T(8,128)} %get-tuple-element.367) | copy-start | bytes 2359300
  648.6 14.1 %collective-permute-start.21 = (f32[256]{0:T(256)S(1)}, f32[256]{0:T(256)S(1)}, u32[]{:S(2)}, u32[]{:S(2)}) collective-permute-start(f32[256]{0:T(256)S(1)} %get-tuple-element.586), channel_id=1, source_target_pairs={{0,4},{4,8},{8,12},{12,16},{16,20},{20,24},{24,28},{28,32},{32,36}... | collective-permute-start | bytes 3080 | tf_op jit(solution)/shard_map/ppermute | solution.py:21
  650.7 12.0 %collective-permute-start.20 = (f32[256]{0:T(256)S(1)}, f32[256]{0:T(256)S(1)}, u32[]{:S(2)}, u32[]{:S(2)}) collective-permute-start(f32[256]{0:T(256)S(1)} %get-tuple-element.585), channel_id=1, source_target_pairs={{4,0},{8,4},{12,8},{16,12},{20,16},{24,20},{28,24},{32,28},{36,32}... | collective-permute-start | bytes 3080 | tf_op jit(solution)/shard_map/ppermute | solution.py:21
  653.1 9.6 %collective-permute-start.23 = (f32[256]{0:T(256)S(1)}, f32[256]{0:T(256)S(1)}, u32[]{:S(2)}, u32[]{:S(2)}) collective-permute-start(f32[256]{0:T(256)S(1)} %get-tuple-element.588), channel_id=1, source_target_pairs={{0,4},{4,8},{8,12},{12,16},{16,20},{20,24},{24,28},{28,32},{32,36}... | collective-permute-start | bytes 3080 | tf_op jit(solution)/shard_map/ppermute | solution.py:21
  658.4 7.0 %collective-permute-start.22 = (f32[256]{0:T(256)S(1)}, f32[256]{0:T(256)S(1)}, u32[]{:S(2)}, u32[]{:S(2)}) collective-permute-start(f32[256]{0:T(256)S(1)} %get-tuple-element.587), channel_id=1, source_target_pairs={{4,0},{8,4},{12,8},{16,12},{20,16},{24,20},{28,24},{32,28},{36,32}... | collective-permute-start | bytes 3080 | tf_op jit(solution)/shard_map/ppermute | solution.py:21
  660.4 5.5 collective-permute-start.15
  (13 other events, 95.4 us)
where the time goes:
time: 679 us; the launch traced here: 668 us
  other arithmetic  259 us (38%)
  local copies, waits for them, and re-layouts  233 us (34%)
  starting transfers between devices  110 us (16%)
  waiting for transfers between devices  35.2 us (5%)
  blocking collectives  21.9 us (3%)
    reshape x4, local copies, waits for them, and re-layouts, per_device(): contact = jnp.zeros((3, displacement[0].size), jnp.float32).at[:, segment...  80.2 us
    scatter-add x4, other arithmetic, per_device(): contact = jnp.zeros((3, displacement[0].size), jnp.float32).at[:, segment...  77.5 us
    ppermute x24, starting transfers between devices, shifted(): lax.ppermute(value, axis, [(source, source + steps) for source in range(f...  73.2 us
    gather x4, local copies, waits for them, and re-layouts, per_device(): points = segment_base + displacement.reshape(3, -1)[:, segment_node]  54.6 us
    add x3, local copies, waits for them, and re-layouts, per_device(): displacement = displacement + TIME_STEP * velocity  49.3 us
    reduce_sum x64, other arithmetic, one_block(): heating = SHORT_GAIN * jnp.sum(pressure * pressure, axis=1)  38 us
    ppermute x24, waiting for transfers between devices, shifted(): lax.ppermute(value, axis, [(source, source + steps) for source in range(f...  32.5 us
    scatter-add x4, other arithmetic, per_device(): jax.ops.segment_sum(segment_heat, tile_slot, num_segments=3 * TILE_DEV)  31 us
  transfers between devices with their start and end apart: 33, of which 9 were waited for; matrix products, arithmetic and copies ran while one was open for 64% of the time, Pallas kernels for 0%

commit v1 on v0

v1 whole, which is shorter than its diff:
```python
import functools

import jax
import jax.numpy as jnp
from jax import lax
from jax.experimental import pallas as pl
from jax.experimental.pallas import tpu as pltpu
from jax.sharding import PartitionSpec as P

SUB = 4
SEG = 128
TILE_DEV = 256
RADIUS = 0.09
PENALTY = 4.0
SHORT_GAIN = 100.0
TIME_STEP = 0.2

CX, CY, ZT = 8, 16, 4
NBLK, CAP, NBIN = 8, 4, 4
NSEG = NBLK * SEG
ROWS = CX * ZT * CY
PIECES = 3
FAR = 1e12
MESH = pl.DeviceIdType.MESH
F32, BF16, I32 = jnp.float32, jnp.bfloat16, jnp.int32


def pieces_of(value):
    parts = []
    for _ in range(PIECES):
        part = value.astype(BF16)
        parts.append(part)
        value = value - part.astype(F32)
    return parts


def lanes_of(shape):
    return lax.broadcasted_iota(I32, shape, len(shape) - 1)


def next_z(value):
    turned = pltpu.roll(value, 127, 2)
    beyond = jnp.concatenate([turned[1:], turned[:1]], axis=0)
    return jnp.where(lanes_of(value.shape) == 127, beyond, turned)


def last_z(value):
    turned = pltpu.roll(value, 1, 2)
    before = jnp.concatenate([turned[-1:], turned[:-1]], axis=0)
    return jnp.where(lanes_of(value.shape) == 0, before, turned)


def spread_row(row):
    return jnp.broadcast_to(row, (SEG, SEG)).T


def kernel(
    disp_in, velo_in, moduli_in, mass_in, tile_in, node_ref, base_ref, bins_ref,
    disp_out, velo_out, heat_out,
    disp, velo, moduli, inverse, tiles,
    one_seg, one_node, lane_col, base_col, tile_lane, tile_row,
    split_disp, split_push, seg_col, seg_row, outgoing, pool, spread,
    push_acc, heat_acc, contact,
    grads, stress, near, far,
    col_out, col_in, corner_out, corner_in,
    layer_force_out, layer_force_in, col_force_out, col_force_in,
    corner_force_out, corner_force_in,
    heat_parts, heat_in, slots,
    in_sem, out_sem, send_sem, recv_sem, point_send, point_recv, heat_send, heat_recv,
):
    dom, own = lax.axis_index("dom"), lax.axis_index("bin")
    doms, bins = lax.axis_size("dom"), lax.axis_size("bin")
    dom_up, dom_low = dom < doms - 1, dom > 0
    bin_up, bin_low = own < bins - 1, own > 0
    diag_up, diag_low = jnp.logical_and(dom_up, bin_up), jnp.logical_and(dom_low, bin_low)

    loads = []
    for z in range(ZT):
        z_at = pl.ds(z * 128, 128)
        loads.append((disp_in.at[:, :, :, z_at], disp.at[:, pl.ds(0, CX), z, pl.ds(8, CY), :]))
        loads.append((tile_in.at[:, :, z_at], tiles.at[:, z]))
        loads.append((moduli_in.at[:, :, :, z_at], moduli.at[:, :, z]))
        loads.append((mass_in.at[:, :, z_at], inverse.at[:, z]))
        loads.append((velo_in.at[:, :, :, z_at], velo.at[:, :, z]))
    loads = [pltpu.make_async_copy(a, b, in_sem.at[i]) for i, (a, b) in enumerate(loads)]
    for load in loads:
        load.start()

    disp[:, CX, :, :, :] = jnp.zeros((3, ZT, 32, 128), F32)
    col_in[...] = jnp.zeros_like(col_in)
    corner_in[...] = jnp.zeros_like(corner_in)
    layer_force_in[...] = jnp.zeros_like(layer_force_in)
    col_force_in[...] = jnp.zeros_like(col_force_in)
    corner_force_in[...] = jnp.zeros_like(corner_force_in)
    heat_in[...] = jnp.zeros_like(heat_in)
    for k in range(6):
        stress[k, 0] = jnp.zeros((ZT, CY, 128), F32)
        stress[k, CX + 1] = jnp.zeros((ZT, CY, 128), F32)
    for p in range(3):
        far[p, CX, :, 0:8, :] = jnp.zeros((ZT, 8, 128), F32)
        seg_row[NBLK] = jnp.full((4, 128), FAR, F32)

    barrier = pltpu.get_barrier_semaphore()
    peers = [(dom, lax.rem(own + i, bins), None) for i in range(1, NBIN)]
    peers += [(dom + 1, own, dom_up), (dom - 1, own, dom_low)]
    peers += [(dom + 1, own + 1, diag_up), (dom - 1, own - 1, diag_low)]
    for to_dom, to_bin, exists in peers:
        def greet(to_dom=to_dom, to_bin=to_bin):
            pl.semaphore_signal(barrier, inc=1, device_id=(to_dom, to_bin), device_id_type=MESH)
        if exists is None:
            greet()
        else:
            pl.when(exists)(greet)

    def fill_slots(step, carry):
        named = [bins_ref[step * NBLK + b] for b in range(NBLK)]
        for k in range(NBIN):
            count = jnp.int32(0)
            found = [jnp.int32(NBLK)] * CAP
            for b in range(NBLK):
                same = named[b] == k
                for rank in range(CAP):
                    found[rank] = jnp.where(
                        jnp.logical_and(same, count == rank), jnp.int32(b), found[rank]
                    )
                count = count + same.astype(I32)
            for rank in range(CAP):
                slots[(step * NBIN + k) * CAP + rank] = found[rank]
        return carry

    lax.fori_loop(0, SUB, fill_slots, 0)

    eye = lax.broadcasted_iota(I32, (SEG, SEG), 0) == lanes_of((SEG, SEG))

    def place_block(b, carry):
        node = node_ref[pl.ds(b, 1), :]
        x, y = lax.shift_right_logical(node, 13), lax.shift_right_logical(node, 9) & 15
        z = lax.shift_right_logical(node, 7) & 3
        row = (x * ZT + z) * CY + y
        lane = node & 127
        at = pl.ds(pl.multiple_of(b * SEG, SEG), SEG)
        row_ids = lax.broadcasted_iota(I32, (ROWS, SEG), 0)
        hits = jnp.where(row_ids == row, 1.0, 0.0).astype(BF16)
        for p in range(PIECES):
            p_at = pl.ds(pl.multiple_of(p * NSEG + b * SEG, SEG), SEG)
            one_seg[:, p_at] = hits
        row_col = spread_row(row.astype(F32))
        ids = lanes_of((SEG, SEG)).astype(F32)
        for part in range(ROWS // 128):
            hits = jnp.where(row_col == ids + float(128 * part), 1.0, 0.0).astype(BF16)
            for p in range(PIECES):
                one_node[at, p * ROWS + part * 128 : p * ROWS + part * 128 + 128] = hits
        lane_col[at, :] = spread_row(lane.astype(F32))
        for c in range(3):
            base_col[c, at, :] = spread_row(base_ref[c, pl.ds(b, 1), :])
        heat_acc[at, :] = jnp.zeros((SEG, SEG), F32)
        return carry

    lax.fori_loop(0, NBLK, place_block, 0)

    for load in loads:
        load.wait()

    def scale(x, carry):
        for k in range(2):
            moduli[k, x] = moduli[k, x] * -0.0625
        inverse[x] = TIME_STEP / inverse[x]
        return carry

    lax.fori_loop(0, CX, scale, 0)

    greeted = jnp.int32(NBIN - 1)
    for _, _, exists in peers[NBIN - 1 :]:
        greeted = greeted + exists.astype(I32)
    pl.semaphore_wait(barrier, greeted)

    def remote(src, dst, index, to_dom, to_bin):
        return pltpu.make_async_remote_copy(
            src_ref=src, dst_ref=dst, send_sem=send_sem.at[index], recv_sem=recv_sem.at[index],
            device_id=(to_dom, to_bin), device_id_type=MESH,
        )

    inner = pl.ds(8, CY)
    layer_copy = remote(disp.at[:, 0, :, inner, :], disp.at[:, CX, :, inner, :], 0, dom - 1, own)
    col_copy = remote(col_out, col_in, 1, dom, own - 1)
    corner_copy = remote(corner_out, corner_in, 2, dom - 1, own - 1)
    layer_force_copy = remote(layer_force_out, layer_force_in, 3, dom + 1, own)
    col_force_copy = remote(col_force_out, col_force_in, 4, dom, own + 1)
    corner_force_copy = remote(corner_force_out, corner_force_in, 5, dom + 1, own + 1)

    def touching(ahead, step, fresh):
        def rows_of(i, carry):
            at = pl.ds(pl.multiple_of(i * 16, 16), 16)
            mine = [seg_col[c, at, :].reshape(2, 8, 128) for c in range(3)]
            named = bins_ref[step * NBLK + i // 8]
            sums = [
                jnp.zeros((2, 8, 128), F32) if fresh else push_acc[c, at, :].reshape(2, 8, 128)
                for c in range(3)
            ]
            heat = heat_acc[at, :].reshape(2, 8, 128)
            for i in ahead:
                for k in range(CAP):
                    slot = i * (NBIN * CAP) + named * CAP + k
                    delta = [mine[c] - spread[slot, c] for c in range(3)]
                    square = delta[0] * delta[0] + delta[1] * delta[1] + delta[2] * delta[2]
                    square = jnp.maximum(square, 1e-30)
                    over = lax.rsqrt(square)
                    pressure = jnp.maximum(RADIUS - square * over, 0.0)
                    weight = pressure * jnp.minimum(over, 1.0 / (0.25 * RADIUS))
                    heat = heat + pressure * pressure
                    sums = [sums[c] + weight * delta[c] for c in range(3)]
            for c in range(3):
                push_acc[c, at, :] = sums[c].reshape(16, 128)
            heat_acc[at, :] = heat.reshape(16, 128)
            return carry

        lax.fori_loop(0, NSEG // 16, rows_of, 0)

    def substep(step, carry):
        parity = lax.rem(step, 2)

        for c in range(3):
            for z in range(ZT):
                corner_out[c * ZT + z : c * ZT + z + 1, :] = disp[c, 0, z, 8:9, :]
                for x in range(CX):
                    col_out[c, z, x : x + 1, :] = disp[c, x, z, 8:9, :]
        pl.when(dom_low)(layer_copy.start)
        pl.when(bin_low)(col_copy.start)
        pl.when(diag_low)(corner_copy.start)

        def split(x, carry):
            for c in range(3):
                value = disp[c, x, :, 8 : 8 + CY, :].reshape(ZT * CY, 128)
                for p, part in enumerate(pieces_of(value)):
                    at = pl.ds(pl.multiple_of(p * ROWS + x * (ZT * CY), ZT * CY), ZT * CY)
                    split_disp[at, c * 128 : c * 128 + 128] = part
            return carry

        lax.fori_loop(0, CX, split, 0)

        def positions(b, carry):
            at = pl.ds(pl.multiple_of(b * SEG, SEG), SEG)
            picked = jnp.dot(one_node[at, :], split_disp[...], preferred_element_type=F32)
            mask = lane_col[at, :] == lanes_of((SEG, SEG)).astype(F32)
            for c in range(3):
                moved = jnp.where(mask, picked[:, c * 128 : c * 128 + 128], 0.0)
                column = base_col[c, at, :] + jnp.sum(moved, axis=1, keepdims=True)
                seg_col[c, at, :] = column
                seg_row[b, c : c + 1, :] = jnp.sum(
                    jnp.where(eye, column, 0.0), axis=0, keepdims=True
                )
            return carry

        lax.fori_loop(0, NBLK, positions, 0)
        for slot in range(NBIN * CAP):
            block = seg_row[slots[step * (NBIN * CAP) + slot]]
            outgoing[slot] = block
            for c in range(3):
                spread[slot, c] = jnp.broadcast_to(block[c : c + 1, :], (8, 128))
        for i in range(1, NBIN):
            point_copy(i, parity).start()

        touching([0], step, True)

        pl.when(dom_up)(layer_copy.wait_recv)
        pl.when(bin_up)(col_copy.wait_recv)
        pl.when(diag_up)(corner_copy.wait_recv)
        for c in range(3):
            for z in range(ZT):
                disp[c, CX, z, 24:25, :] = corner_in[c * ZT + z : c * ZT + z + 1, :]
                for x in range(CX):
                    disp[c, x, z, 24:25, :] = col_in[c, z, x : x + 1, :]

        def corners(x, carry):
            for c in range(3):
                low, high = disp[c, x, :, 8:24, :], disp[c, x, :, 9:25, :]
                total, gap = low + high, high - low
                total_next, gap_next = next_z(total), next_z(gap)
                grads[c, 0, x] = total + total_next
                grads[c, 1, x] = gap + gap_next
                grads[c, 2, x] = total_next - total
            return carry

        lax.fori_loop(0, CX + 1, corners, 0)

        def stresses(x, carry):
            g = [
                [grads[c, 0, x + 1] - grads[c, 0, x]]
                + [grads[c, q, x] + grads[c, q, x + 1] for q in (1, 2)]
                for c in range(3)
            ]
            lame, shear = moduli[0, x], moduli[1, x]
            volume = lame * (g[0][0] + g[1][1] + g[2][2])
            for p in range(3):
                stress[p, x + 1] = shear * (g[p][p] + g[p][p]) + volume
            stress[3, x + 1] = shear * (g[0][1] + g[1][0])
            stress[4, x + 1] = shear * (g[0][2] + g[2][0])
            stress[5, x + 1] = shear * (g[1][2] + g[2][1])
            return carry

        lax.fori_loop(0, CX, stresses, 0)

        def forces(x, carry):
            for p, (kx, ky, kz) in enumerate(((0, 3, 4), (3, 1, 5), (4, 5, 2))):
                along_x = stress[kx, x] - stress[kx, x + 1]
                along_y = stress[ky, x] + stress[ky, x + 1]
                along_z = stress[kz, x] + stress[kz, x + 1]
                minus, plus = along_x - along_y, along_x + along_y
                near[p, x] = (minus - along_z) + last_z(minus + along_z)
                far[p, x, :, 8:24, :] = (plus - along_z) + last_z(plus + along_z)
            return carry

        lax.fori_loop(0, CX + 1, forces, 0)
        for p in range(3):
            layer_force_out[p] = near[p, CX] + far[p, CX, :, 7:23, :]
            for z in range(ZT):
                corner_force_out[p * ZT + z : p * ZT + z + 1, :] = far[p, CX, z, 23:24, :]
                for x in range(CX):
                    col_force_out[p, z, x : x + 1, :] = far[p, x, z, 23:24, :]
        pl.when(dom_up)(layer_force_copy.start)
        pl.when(bin_up)(col_force_copy.start)
        pl.when(diag_up)(corner_force_copy.start)

        for i in range(1, NBIN):
            point_copy(i, parity).wait_recv()

        def spread_slot(slot, carry):
            for i in range(1, NBIN):
                block = pool[parity, lax.rem(own + i, bins), slot]
                for c in range(3):
                    spread[i * (NBIN * CAP) + slot, c] = jnp.broadcast_to(
                        block[c : c + 1, :], (8, 128)
                    )
            return carry

        lax.fori_loop(0, NBIN * CAP, spread_slot, 0)
        touching(range(1, NBIN), step, False)

        def lay_push(b, carry):
            at = pl.ds(pl.multiple_of(b * SEG, SEG), SEG)
            mask = lane_col[at, :] == lanes_of((SEG, SEG)).astype(F32)
            for c in range(3):
                total = jnp.sum(push_acc[c, at, :], axis=1, keepdims=True)
                laid = jnp.where(mask, PENALTY * total, 0.0)
                for p, part in enumerate(pieces_of(laid)):
                    p_at = pl.ds(pl.multiple_of(p * NSEG + b * SEG, SEG), SEG)
                    split_push[p_at, c * 128 : c * 128 + 128] = part
            return carry

        lax.fori_loop(0, NBLK, lay_push, 0)
        pushed = jnp.dot(one_seg[...], split_push[...], preferred_element_type=F32)
        for c in range(3):
            contact[c] = pushed[:, c * 128 : c * 128 + 128]

        pl.when(dom_low)(layer_force_copy.wait_recv)
        pl.when(bin_low)(col_force_copy.wait_recv)
        pl.when(diag_low)(corner_force_copy.wait_recv)
        for p in range(3):
            near[p, 0] = near[p, 0] + layer_force_in[p]
            for z in range(ZT):
                near[p, 0, z, 0:1, :] = (
                    near[p, 0, z, 0:1, :] + corner_force_in[p * ZT + z : p * ZT + z + 1, :]
                )
                for x in range(CX):
                    far[p, x, z, 7:8, :] = col_force_in[p, z, x : x + 1, :]
        pl.when(dom_low)(layer_copy.wait_send)
        pl.when(bin_low)(col_copy.wait_send)
        pl.when(diag_low)(corner_copy.wait_send)
        pl.when(dom_up)(layer_force_copy.wait_send)
        pl.when(bin_up)(col_force_copy.wait_send)
        pl.when(diag_up)(corner_force_copy.wait_send)
        for i in range(1, NBIN):
            point_copy(i, parity).wait_send()

        def advance(x, carry):
            for p in range(3):
                at = pl.ds(pl.multiple_of(x * (ZT * CY), ZT * CY), ZT * CY)
                force = near[p, x] + far[p, x, :, 7:23, :]
                force = force + contact[p, at, :].reshape(ZT, CY, 128)
                moved = velo[p, x] + force * inverse[x]
                velo[p, x] = moved
                disp[p, x, :, 8:24, :] = disp[p, x, :, 8:24, :] + TIME_STEP * moved
            return carry

        lax.fori_loop(0, CX, advance, 0)
        return carry

    def point_copy(i, parity):
        return pltpu.make_async_remote_copy(
            src_ref=outgoing, dst_ref=pool.at[parity, own],
            send_sem=point_send.at[i - 1], recv_sem=point_recv.at[parity, i - 1],
            device_id=(dom, lax.rem(own + i, bins)), device_id_type=MESH,
        )

    lax.fori_loop(0, SUB, substep, 0)

    stores = []
    for z in range(ZT):
        z_at = pl.ds(z * 128, 128)
        stores.append((disp.at[:, pl.ds(0, CX), z, inner, :], disp_out.at[:, :, :, z_at]))
        stores.append((velo.at[:, :, z], velo_out.at[:, :, :, z_at]))
    stores = [pltpu.make_async_copy(a, b, out_sem.at[i]) for i, (a, b) in enumerate(stores)]
    for store in stores:
        store.start()

    device = dom * bins + own

    def split_tiles(x, carry):
        offset = tiles[x] - device * TILE_DEV + bins * TILE_DEV
        side = lax.shift_right_logical(offset, 10)
        row = side * 2 + (lax.shift_right_logical(offset, 7) & 1)
        at = pl.ds(pl.multiple_of(x * (ZT * CY), ZT * CY), ZT * CY)
        split_disp[at, 0:128] = row.astype(F32).astype(BF16).reshape(ZT * CY, 128)
        lane = (offset & 127).astype(F32).astype(BF16)
        split_disp[at, 128:256] = lane.reshape(ZT * CY, 128)
        return carry

    lax.fori_loop(0, CX, split_tiles, 0)

    def lay_heat(b, carry):
        at = pl.ds(pl.multiple_of(b * SEG, SEG), SEG)
        picked = jnp.dot(
            one_node[at, 0:ROWS], split_disp[0:ROWS, 0:256], preferred_element_type=F32
        )
        ids = lanes_of((SEG, SEG)).astype(F32)
        mask = lane_col[at, :] == ids
        row_col = jnp.sum(jnp.where(mask, picked[:, 0:128], 0.0), axis=1, keepdims=True)
        lane = jnp.sum(jnp.where(mask, picked[:, 128:256], 0.0), axis=1, keepdims=True)
        tile_row[b, 0:1, :] = jnp.sum(jnp.where(eye, row_col, 0.0), axis=0, keepdims=True)
        total = SHORT_GAIN * jnp.sum(heat_acc[at, :], axis=1, keepdims=True)
        laid = jnp.where(lane == ids, total, 0.0)
        for p, part in enumerate(pieces_of(laid)):
            tile_lane[p, at, :] = part
        return carry

    lax.fori_loop(0, NBLK, lay_heat, 0)
    on_tiles = jnp.zeros((16, 128), F32)
    for b in range(NBLK):
        ids = lax.broadcasted_iota(I32, (16, SEG), 0).astype(F32)
        hits = jnp.where(ids == tile_row[b, 0:1, :], 1.0, 0.0).astype(BF16)
        for p in range(PIECES):
            on_tiles = on_tiles + jnp.dot(
                hits, tile_lane[p, b * SEG : (b + 1) * SEG, :], preferred_element_type=F32
            )
    for side in range(3):
        heat_parts[side, 0:2, :] = on_tiles[side * 2 : side * 2 + 2, :]

    def heat_copy(index, to_dom):
        return pltpu.make_async_remote_copy(
            src_ref=heat_parts.at[2 * index], dst_ref=heat_in.at[index],
            send_sem=heat_send.at[index], recv_sem=heat_recv.at[index],
            device_id=(to_dom, own), device_id_type=MESH,
        )

    to_low, to_up = heat_copy(0, dom - 1), heat_copy(1, dom + 1)
    pl.when(dom_low)(to_low.start)
    pl.when(dom_up)(to_up.start)
    pl.when(dom_up)(to_low.wait_recv)
    pl.when(dom_low)(to_up.wait_recv)
    heat_out[...] = heat_parts[1, 0:2, :] + heat_in[0, 0:2, :] + heat_in[1, 0:2, :]
    pl.when(dom_low)(to_low.wait_send)
    pl.when(dom_up)(to_up.wait_send)
    for store in stores:
        store.wait()


def per_device(displacement, velocity, moduli, nodal_mass, node, base, contact_bin, element_tile):
    anywhere = pl.BlockSpec(memory_space=pl.ANY)
    vmem = pl.BlockSpec(memory_space=pltpu.VMEM)
    smem = pl.BlockSpec(memory_space=pltpu.SMEM)
    dma, vec = pltpu.SemaphoreType.DMA, pltpu.VMEM
    slab = (ZT, CY, 128)
    scratch = [
        vec((3, CX + 1, ZT, 32, 128), F32),
        vec((3, CX) + slab, F32),
        vec((2, CX) + slab, F32),
        vec((CX,) + slab, F32),
        vec((CX,) + slab, I32),
        vec((ROWS, PIECES * NSEG), BF16),
        vec((NSEG, PIECES * ROWS), BF16),
        vec((NSEG, 128), F32),
        vec((3, NSEG, 128), F32),
        vec((PIECES, NSEG, 128), BF16),
        vec((NBLK, 8, 128), F32),
        vec((PIECES * ROWS, 384), BF16),
        vec((PIECES * NSEG, 384), BF16),
        vec((3, NSEG, 128), F32),
        vec((NBLK + 1, 4, 128), F32),
        vec((NBIN * CAP, 4, 128), F32),
        vec((2, NBIN, NBIN * CAP, 4, 128), F32),
        vec((NBIN * NBIN * CAP, 3, 8, 128), F32),
        vec((3, NSEG, 128), F32),
        vec((NSEG, 128), F32),
        vec((3, ROWS, 128), F32),
        vec((3, 3, CX + 1) + slab, F32),
        vec((6, CX + 2) + slab, F32),
        vec((3, CX + 1) + slab, F32),
        vec((3, CX + 1, ZT, 32, 128), F32),
        vec((3, ZT, CX, 128), F32),
        vec((3, ZT, CX, 128), F32),
        vec((16, 128), F32),
        vec((16, 128), F32),
        vec((3,) + slab, F32),
        vec((3,) + slab, F32),
        vec((3, ZT, CX, 128), F32),
        vec((3, ZT, CX, 128), F32),
        vec((16, 128), F32),
        vec((16, 128), F32),
        vec((3, 8, 128), F32),
        vec((2, 8, 128), F32),
        pltpu.SMEM((SUB * NBIN * CAP,), I32),
        dma((5 * ZT,)),
        dma((2 * ZT,)),
        dma((6,)),
        dma((6,)),
        dma((NBIN - 1,)),
        dma((2, NBIN - 1)),
        dma((2,)),
        dma((2,)),
    ]
    new_displacement, new_velocity, heat = pl.pallas_call(
        kernel,
        out_shape=(
            jax.ShapeDtypeStruct(displacement.shape, F32),
            jax.ShapeDtypeStruct(velocity.shape, F32),
            jax.ShapeDtypeStruct((2, 128), F32),
        ),
        in_specs=[anywhere] * 5 + [vmem, vmem, smem],
        out_specs=(anywhere, anywhere, vmem),
        scratch_shapes=scratch,
        compiler_params=pltpu.CompilerParams(
            collective_id=0, has_side_effects=True, vmem_limit_bytes=56 << 20
        ),
        name="module_substeps",
    )(
        displacement, velocity, moduli, nodal_mass, element_tile,
        node.reshape(NBLK, SEG), base.reshape(3, NBLK, SEG), contact_bin.reshape(-1),
    )
    return new_displacement, new_velocity, heat.reshape(-1)


def solution(mesh):
    placed = (
        P(None, "dom", "bin", None),
        P(None, "dom", "bin", None),
        P(None, "dom", "bin", None),
        P("dom", "bin", None),
        P(("dom", "bin")),
        P(None, ("dom", "bin")),
        P(None, ("dom", "bin"), None),
        P("dom", "bin", None),
    )
    return jax.shard_map(
        per_device,
        mesh=mesh,
        in_specs=placed,
        out_specs=(P(None, "dom", "bin", None), P(None, "dom", "bin", None), P(("dom", "bin"))),
        check_vma=False,
    )
```

time: 679 us -> 94.9 us (0.14); the launches traced: 668 us -> 94.2 us
  other arithmetic: 259 us -> 0.66 us
  local copies, waits for them, and re-layouts: 233 us -> 6.2 us
  starting transfers between devices: 110 us -> 0 us
  Pallas kernels: 0 us -> 86.7 us
  waiting for transfers between devices: 35.2 us -> 0 us
  blocking collectives: 21.9 us -> 0 us
    scatter-add x8 -> x0, other arithmetic: 109 us -> none  [the longest x4 77.5 us: per_device(): contact = jnp.zeros((3, displacement[0].size), jnp.float32).at[:, segment...]
    reduce_sum x198 -> x0, other arithmetic: 92.3 us -> none  [the longest x64 38 us: one_block(): heating = SHORT_GAIN * jnp.sum(pressure * pressure, axis=1)]
    pallas_call x0 -> x1, Pallas kernels: none -> 86.7 us  [per_device(): pl.pallas_call(kernel, out_shape=(jax.ShapeDtypeStruct(displacement.shape...]
    reshape x16 -> x1, local copies, waits for them, and re-layouts: 83.3 us -> 0.6 us  [per_device(): contact_bin.reshape(-1)]
    ppermute x24 -> x0, starting transfers between devices: 73.2 us -> none  [shifted(): lax.ppermute(value, axis, [(source, source + steps) for source in range(f...]
    gather x5 -> x0, local copies, waits for them, and re-layouts: 60.8 us -> none  [the longest x4 54.6 us: per_device(): points = segment_base + displacement.reshape(3, -1)[:, segment_node]]
    add x3 -> x0, local copies, waits for them, and re-layouts: 49.3 us -> none  [per_device(): displacement = displacement + TIME_STEP * velocity]
    all_to_all x9 -> x0, starting transfers between devices: 36.3 us -> none  [the longest x4 18.3 us: per_device(): lax.all_to_all(results, 'bin', split_axis=0, concat_axis=0, tiled=True)]
  transfers between devices with their start and end apart: 33 -> 0, of which waited for: 9 -> 0; matrix products, arithmetic and copies ran while one was open for 64% -> 0% of each run, Pallas kernels for 0% -> 0%
where the time goes in v1:
time: 94.9 us; the launch traced here: 94.2 us
  Pallas kernels  86.7 us (91%)
  local copies, waits for them, and re-layouts  6.2 us (7%)
    pallas_call x1, Pallas kernels, per_device(): pl.pallas_call(kernel, out_shape=(jax.ShapeDtypeStruct(displacement.shape...  86.7 us
    unnamed x11, local copies, waits for them, and re-layouts  5.6 us

profile of v1, /device:TPU:39, one launch (start us, length us, event | category | flops | bytes accessed | tf_op | source)
XLA Modules:
  0.0 94.2 jit_solution(15339340702512242593)
XLA Ops:
  0.6 0.0 copy-start.1
  0.6 0.5 broadcast.3
  1.2 0.2 copy-done.1
  1.3 0.7 reduce.3
  2.0 0.6 reshape.20.bins_ref
  2.6 1.3 %copy.13 = f32[1,3,8,128]{3,2,1,0:T(8,128)} copy(f32[1,3,8,128]{3,1,2,0:T(4,128)} %bitcast.8) | data formatting | bytes 24576
  3.9 86.7 %module_substeps.1 = (f32[3,8,16,512]{3,2,1,0:T(8,128)}, f32[3,8,16,512]{3,2,1,0:T(8,128)}, f32[2,128]{1,0:T(2,128)}) custom-call(f32[3,8,16,512]{3,2,1,0:T(8,128)} %disp_in.1, f32[3,8,16,512]{3,2,1,0:T(8,128)} %velo_in.1, f32[2,8,16,512]{3,2,1,0:T(8,128)} %moduli_in.1, f32[8,16,512]{2,1,0:T(8,128)} %mass_in.1, s32[8,16,512]{2,1,0:T(8,128)} %tile_in.1, ...), custom_call_target="tpu_custom_call" | custom-call | tf_op jit(solution)/shard_map/module_substeps/pallas_call | solution.py:521
  90.6 0.0 copy-start
  90.6 2.2 %copy.17 = f32[3,8,16,512]{3,2,1,0:T(8,128)} copy(f32[3,8,16,512]{3,2,1,0:T(8,128)} %get-tuple-element.12) | data formatting | bytes 1572864
  92.7 0.0 copy-done
  92.7 0.0 copy-start.2
  92.7 0.9 copy.18
  93.6 0.0 copy-done.2
  93.6 0.6 copy.19
Async XLA Ops:
  0.6 0.7 copy-start.1
  90.6 2.2 %copy-start = (f32[3,8,16,512]{3,2,1,0:T(8,128)S(1)}, f32[3,8,16,512]{3,2,1,0:T(8,128)}, u32[]{:S(2)}) copy-start(f32[3,8,16,512]{3,2,1,0:T(8,128)} %get-tuple-element.13) | copy-start | bytes 2359300
  92.7 0.9 copy-start.2

commit v2 on v1

--- a/solution.py
+++ b/solution.py
@@ -19,7 +19,8 @@
 NBLK, CAP, NBIN = 8, 4, 4
 NSEG = NBLK * SEG
 ROWS = CX * ZT * CY
-PIECES = 3
+PIECES = 2
+WIDE = 384
 FAR = 1e12
 MESH = pl.DeviceIdType.MESH
 F32, BF16, I32 = jnp.float32, jnp.bfloat16, jnp.int32
@@ -56,17 +57,17 @@
 
 def kernel(
     disp_in, velo_in, moduli_in, mass_in, tile_in, node_ref, base_ref, bins_ref,
-    disp_out, velo_out, heat_out,
-    disp, velo, moduli, inverse, tiles,
+    disp_out, velo, heat_out,
+    disp, moduli, inverse, tiles,
     one_seg, one_node, lane_col, base_col, tile_lane, tile_row,
     split_disp, split_push, seg_col, seg_row, outgoing, pool, spread,
-    push_acc, heat_acc, contact,
+    push_acc, heat_acc, picked, pushed,
     grads, stress, near, far,
     col_out, col_in, corner_out, corner_in,
     layer_force_out, layer_force_in, col_force_out, col_force_in,
     corner_force_out, corner_force_in,
     heat_parts, heat_in, slots,
-    in_sem, out_sem, send_sem, recv_sem, point_send, point_recv, heat_send, heat_recv,
+    in_sem, send_sem, recv_sem, point_send, point_recv, heat_send, heat_recv,
 ):
     dom, own = lax.axis_index("dom"), lax.axis_index("bin")
     doms, bins = lax.axis_size("dom"), lax.axis_size("bin")
@@ -113,7 +114,7 @@
             pl.when(exists)(greet)
 
     def fill_slots(step, carry):
-        named = [bins_ref[step * NBLK + b] for b in range(NBLK)]
+        named = [bins_ref[step, 0, b] for b in range(NBLK)]
         for k in range(NBIN):
             count = jnp.int32(0)
             found = [jnp.int32(NBLK)] * CAP
@@ -140,19 +141,15 @@
         lane = node & 127
         at = pl.ds(pl.multiple_of(b * SEG, SEG), SEG)
         row_ids = lax.broadcasted_iota(I32, (ROWS, SEG), 0)
-        hits = jnp.where(row_ids == row, 1.0, 0.0).astype(BF16)
-        for p in range(PIECES):
-            p_at = pl.ds(pl.multiple_of(p * NSEG + b * SEG, SEG), SEG)
-            one_seg[:, p_at] = hits
+        one_seg[:, at] = jnp.where(row_ids == row, 1.0, 0.0).astype(BF16)
         row_col = spread_row(row.astype(F32))
         ids = lanes_of((SEG, SEG)).astype(F32)
         for part in range(ROWS // 128):
             hits = jnp.where(row_col == ids + float(128 * part), 1.0, 0.0).astype(BF16)
-            for p in range(PIECES):
-                one_node[at, p * ROWS + part * 128 : p * ROWS + part * 128 + 128] = hits
+            one_node[at, part * 128 : part * 128 + 128] = hits
         lane_col[at, :] = spread_row(lane.astype(F32))
         for c in range(3):
-            base_col[c, at, :] = spread_row(base_ref[c, pl.ds(b, 1), :])
+            base_col[c, at, :] = spread_row(base_ref[c : c + 1, at])
         heat_acc[at, :] = jnp.zeros((SEG, SEG), F32)
         return carry
 
@@ -192,7 +189,7 @@
         def rows_of(i, carry):
             at = pl.ds(pl.multiple_of(i * 16, 16), 16)
             mine = [seg_col[c, at, :].reshape(2, 8, 128) for c in range(3)]
-            named = bins_ref[step * NBLK + i // 8]
+            named = bins_ref[step, 0, i // 8]
             sums = [
                 jnp.zeros((2, 8, 128), F32) if fresh else push_acc[c, at, :].reshape(2, 8, 128)
                 for c in range(3)
@@ -228,30 +225,34 @@
         pl.when(bin_low)(col_copy.start)
         pl.when(diag_low)(corner_copy.start)
 
-        def split(x, carry):
-            for c in range(3):
-                value = disp[c, x, :, 8 : 8 + CY, :].reshape(ZT * CY, 128)
-                for p, part in enumerate(pieces_of(value)):
-                    at = pl.ds(pl.multiple_of(p * ROWS + x * (ZT * CY), ZT * CY), ZT * CY)
-                    split_disp[at, c * 128 : c * 128 + 128] = part
-            return carry
-
-        lax.fori_loop(0, CX, split, 0)
-
-        def positions(b, carry):
-            at = pl.ds(pl.multiple_of(b * SEG, SEG), SEG)
-            picked = jnp.dot(one_node[at, :], split_disp[...], preferred_element_type=F32)
-            mask = lane_col[at, :] == lanes_of((SEG, SEG)).astype(F32)
-            for c in range(3):
-                moved = jnp.where(mask, picked[:, c * 128 : c * 128 + 128], 0.0)
-                column = base_col[c, at, :] + jnp.sum(moved, axis=1, keepdims=True)
-                seg_col[c, at, :] = column
-                seg_row[b, c : c + 1, :] = jnp.sum(
-                    jnp.where(eye, column, 0.0), axis=0, keepdims=True
-                )
-            return carry
-
-        lax.fori_loop(0, NBLK, positions, 0)
+        def split(pair, carry):
+            for x in (2 * pair, 2 * pair + 1):
+                at = pl.ds(pl.multiple_of(x * (ZT * CY), ZT * CY), ZT * CY)
+                for c in range(3):
+                    value = disp[c, x, :, 8 : 8 + CY, :].reshape(ZT * CY, 128)
+                    for p, part in enumerate(pieces_of(value)):
+                        split_disp[at, p * WIDE + c * 128 : p * WIDE + c * 128 + 128] = part
+            return carry
+
+        lax.fori_loop(0, CX // 2, split, 0)
+        picked[...] = jnp.dot(one_node[...], split_disp[...], preferred_element_type=F32)
+
+        def positions(pair, carry):
+            for b in (2 * pair, 2 * pair + 1):
+                at = pl.ds(pl.multiple_of(b * SEG, SEG), SEG)
+                mask = lane_col[at, :] == lanes_of((SEG, SEG)).astype(F32)
+                for c in range(3):
+                    value = picked[at, c * 128 : c * 128 + 128]
+                    value = value + picked[at, WIDE + c * 128 : WIDE + c * 128 + 128]
+                    moved = jnp.where(mask, value, 0.0)
+                    column = base_col[c, at, :] + jnp.sum(moved, axis=1, keepdims=True)
+                    seg_col[c, at, :] = column
+                    seg_row[b, c : c + 1, :] = jnp.sum(
+                        jnp.where(eye, column, 0.0), axis=0, keepdims=True
+                    )
+            return carry
+
+        lax.fori_loop(0, NBLK // 2, positions, 0)
         for slot in range(NBIN * CAP):
             block = seg_row[slots[step * (NBIN * CAP) + slot]]
             outgoing[slot] = block
@@ -271,17 +272,18 @@
                 for x in range(CX):
                     disp[c, x, z, 24:25, :] = col_in[c, z, x : x + 1, :]
 
-        def corners(x, carry):
-            for c in range(3):
-                low, high = disp[c, x, :, 8:24, :], disp[c, x, :, 9:25, :]
-                total, gap = low + high, high - low
-                total_next, gap_next = next_z(total), next_z(gap)
-                grads[c, 0, x] = total + total_next
-                grads[c, 1, x] = gap + gap_next
-                grads[c, 2, x] = total_next - total
-            return carry
-
-        lax.fori_loop(0, CX + 1, corners, 0)
+        def corners(part, carry):
+            for x in [3 * part + i for i in range(3)]:
+                for c in range(3):
+                    low, high = disp[c, x, :, 8:24, :], disp[c, x, :, 9:25, :]
+                    total, gap = low + high, high - low
+                    total_next, gap_next = next_z(total), next_z(gap)
+                    grads[c, 0, x] = total + total_next
+                    grads[c, 1, x] = gap + gap_next
+                    grads[c, 2, x] = total_next - total
+            return carry
+
+        lax.fori_loop(0, (CX + 1) // 3, corners, 0)
 
         def stresses(x, carry):
             g = [
@@ -300,17 +302,18 @@
 
         lax.fori_loop(0, CX, stresses, 0)
 
-        def forces(x, carry):
-            for p, (kx, ky, kz) in enumerate(((0, 3, 4), (3, 1, 5), (4, 5, 2))):
-                along_x = stress[kx, x] - stress[kx, x + 1]
-                along_y = stress[ky, x] + stress[ky, x + 1]
-                along_z = stress[kz, x] + stress[kz, x + 1]
-                minus, plus = along_x - along_y, along_x + along_y
-                near[p, x] = (minus - along_z) + last_z(minus + along_z)
-                far[p, x, :, 8:24, :] = (plus - along_z) + last_z(plus + along_z)
-            return carry
-
-        lax.fori_loop(0, CX + 1, forces, 0)
+        def forces(part, carry):
+            for x in [3 * part + i for i in range(3)]:
+                for p, (kx, ky, kz) in enumerate(((0, 3, 4), (3, 1, 5), (4, 5, 2))):
+                    along_x = stress[kx, x] - stress[kx, x + 1]
+                    along_y = stress[ky, x] + stress[ky, x + 1]
+                    along_z = stress[kz, x] + stress[kz, x + 1]
+                    minus, plus = along_x - along_y, along_x + along_y
+                    near[p, x] = (minus - along_z) + last_z(minus + along_z)
+                    far[p, x, :, 8:24, :] = (plus - along_z) + last_z(plus + along_z)
+            return carry
+
+        lax.fori_loop(0, (CX + 1) // 3, forces, 0)
         for p in range(3):
             layer_force_out[p] = near[p, CX] + far[p, CX, :, 7:23, :]
             for z in range(ZT):
@@ -336,21 +339,19 @@
         lax.fori_loop(0, NBIN * CAP, spread_slot, 0)
         touching(range(1, NBIN), step, False)
 
-        def lay_push(b, carry):
-            at = pl.ds(pl.multiple_of(b * SEG, SEG), SEG)
-            mask = lane_col[at, :] == lanes_of((SEG, SEG)).astype(F32)
-            for c in range(3):
-                total = jnp.sum(push_acc[c, at, :], axis=1, keepdims=True)
-                laid = jnp.where(mask, PENALTY * total, 0.0)
-                for p, part in enumerate(pieces_of(laid)):
-                    p_at = pl.ds(pl.multiple_of(p * NSEG + b * SEG, SEG), SEG)
-                    split_push[p_at, c * 128 : c * 128 + 128] = part
-            return carry
-
-        lax.fori_loop(0, NBLK, lay_push, 0)
-        pushed = jnp.dot(one_seg[...], split_push[...], preferred_element_type=F32)
-        for c in range(3):
-            contact[c] = pushed[:, c * 128 : c * 128 + 128]
+        def lay_push(pair, carry):
+            for b in (2 * pair, 2 * pair + 1):
+                at = pl.ds(pl.multiple_of(b * SEG, SEG), SEG)
+                mask = lane_col[at, :] == lanes_of((SEG, SEG)).astype(F32)
+                for c in range(3):
+                    total = jnp.sum(push_acc[c, at, :], axis=1, keepdims=True)
+                    laid = jnp.where(mask, PENALTY * total, 0.0)
+                    for p, part in enumerate(pieces_of(laid)):
+                        split_push[at, p * WIDE + c * 128 : p * WIDE + c * 128 + 128] = part
+            return carry
+
+        lax.fori_loop(0, NBLK // 2, lay_push, 0)
+        pushed[...] = jnp.dot(one_seg[...], split_push[...], preferred_element_type=F32)
 
         pl.when(dom_low)(layer_force_copy.wait_recv)
         pl.when(bin_low)(col_force_copy.wait_recv)
@@ -376,10 +377,14 @@
             for p in range(3):
                 at = pl.ds(pl.multiple_of(x * (ZT * CY), ZT * CY), ZT * CY)
                 force = near[p, x] + far[p, x, :, 7:23, :]
-                force = force + contact[p, at, :].reshape(ZT, CY, 128)
+                for part in range(PIECES):
+                    column = part * WIDE + p * 128
+                    force = force + pushed[at, column : column + 128].reshape(ZT, CY, 128)
                 moved = velo[p, x] + force * inverse[x]
                 velo[p, x] = moved
-                disp[p, x, :, 8:24, :] = disp[p, x, :, 8:24, :] + TIME_STEP * moved
+                moved = disp[p, x, :, 8:24, :] + TIME_STEP * moved
+                disp[p, x, :, 8:24, :] = moved
+                disp_out[p, x] = moved
             return carry
 
         lax.fori_loop(0, CX, advance, 0)
@@ -393,15 +398,6 @@
         )
 
     lax.fori_loop(0, SUB, substep, 0)
-
-    stores = []
-    for z in range(ZT):
-        z_at = pl.ds(z * 128, 128)
-        stores.append((disp.at[:, pl.ds(0, CX), z, inner, :], disp_out.at[:, :, :, z_at]))
-        stores.append((velo.at[:, :, z], velo_out.at[:, :, :, z_at]))
-    stores = [pltpu.make_async_copy(a, b, out_sem.at[i]) for i, (a, b) in enumerate(stores)]
-    for store in stores:
-        store.start()
 
     device = dom * bins + own
 
@@ -420,7 +416,7 @@
     def lay_heat(b, carry):
         at = pl.ds(pl.multiple_of(b * SEG, SEG), SEG)
         picked = jnp.dot(
-            one_node[at, 0:ROWS], split_disp[0:ROWS, 0:256], preferred_element_type=F32
+            one_node[at, :], split_disp[:, 0:256], preferred_element_type=F32
         )
         ids = lanes_of((SEG, SEG)).astype(F32)
         mask = lane_col[at, :] == ids
@@ -460,30 +456,41 @@
     heat_out[...] = heat_parts[1, 0:2, :] + heat_in[0, 0:2, :] + heat_in[1, 0:2, :]
     pl.when(dom_low)(to_low.wait_send)
     pl.when(dom_up)(to_up.wait_send)
+
+
+def deliver(disp, velo, heat, disp_out, velo_out, heat_out, sem):
+    stores = [(heat, heat_out)]
+    for z in range(ZT):
+        z_at = pl.ds(z * 128, 128)
+        stores.append((disp.at[:, :, z], disp_out.at[:, :, :, z_at]))
+        stores.append((velo.at[:, :, z], velo_out.at[:, :, :, z_at]))
+    stores = [pltpu.make_async_copy(a, b, sem.at[i]) for i, (a, b) in enumerate(stores)]
+    for store in stores:
+        store.start()
     for store in stores:
         store.wait()
 
 
 def per_device(displacement, velocity, moduli, nodal_mass, node, base, contact_bin, element_tile):
     anywhere = pl.BlockSpec(memory_space=pl.ANY)
+    hbm = pl.BlockSpec(memory_space=pltpu.HBM)
     vmem = pl.BlockSpec(memory_space=pltpu.VMEM)
     smem = pl.BlockSpec(memory_space=pltpu.SMEM)
     dma, vec = pltpu.SemaphoreType.DMA, pltpu.VMEM
     slab = (ZT, CY, 128)
     scratch = [
         vec((3, CX + 1, ZT, 32, 128), F32),
-        vec((3, CX) + slab, F32),
         vec((2, CX) + slab, F32),
         vec((CX,) + slab, F32),
         vec((CX,) + slab, I32),
-        vec((ROWS, PIECES * NSEG), BF16),
-        vec((NSEG, PIECES * ROWS), BF16),
+        vec((ROWS, NSEG), BF16),
+        vec((NSEG, ROWS), BF16),
         vec((NSEG, 128), F32),
         vec((3, NSEG, 128), F32),
         vec((PIECES, NSEG, 128), BF16),
         vec((NBLK, 8, 128), F32),
-        vec((PIECES * ROWS, 384), BF16),
-        vec((PIECES * NSEG, 384), BF16),
+        vec((ROWS, PIECES * WIDE), BF16),
+        vec((NSEG, PIECES * WIDE), BF16),
         vec((3, NSEG, 128), F32),
         vec((NBLK + 1, 4, 128), F32),
         vec((NBIN * CAP, 4, 128), F32),
@@ -491,7 +498,8 @@
         vec((NBIN * NBIN * CAP, 3, 8, 128), F32),
         vec((3, NSEG, 128), F32),
         vec((NSEG, 128), F32),
-        vec((3, ROWS, 128), F32),
+        vec((NSEG, PIECES * WIDE), F32),
+        vec((ROWS, PIECES * WIDE), F32),
         vec((3, 3, CX + 1) + slab, F32),
         vec((6, CX + 2) + slab, F32),
         vec((3, CX + 1) + slab, F32),
@@ -510,7 +518,6 @@
         vec((2, 8, 128), F32),
         pltpu.SMEM((SUB * NBIN * CAP,), I32),
         dma((5 * ZT,)),
-        dma((2 * ZT,)),
         dma((6,)),
         dma((6,)),
         dma((NBIN - 1,)),
@@ -518,24 +525,36 @@
         dma((2,)),
         dma((2,)),
     ]
+    results = pl.pallas_call(
+        kernel,
+        out_shape=(
+            pltpu.VMEM((3, CX) + slab, F32),
+            pltpu.VMEM((3, CX) + slab, F32),
+            pltpu.VMEM((2, 128), F32),
+        ),
+        in_specs=[hbm] * 5 + [vmem, vmem, smem],
+        out_specs=(vmem, vmem, vmem),
+        scratch_shapes=scratch,
+        compiler_params=pltpu.CompilerParams(
+            collective_id=0, has_side_effects=True, vmem_limit_bytes=65339392
+        ),
+        name="module_substeps",
+    )(
+        displacement, velocity, moduli, nodal_mass, element_tile,
+        node.reshape(NBLK, SEG), base, contact_bin.transpose(0, 2, 1),
+    )
     new_displacement, new_velocity, heat = pl.pallas_call(
-        kernel,
+        deliver,
         out_shape=(
             jax.ShapeDtypeStruct(displacement.shape, F32),
             jax.ShapeDtypeStruct(velocity.shape, F32),
             jax.ShapeDtypeStruct((2, 128), F32),
         ),
-        in_specs=[anywhere] * 5 + [vmem, vmem, smem],
-        out_specs=(anywhere, anywhere, vmem),
-        scratch_shapes=scratch,
-        compiler_params=pltpu.CompilerParams(
-            collective_id=0, has_side_effects=True, vmem_limit_bytes=56 << 20
-        ),
-        name="module_substeps",
-    )(
-        displacement, velocity, moduli, nodal_mass, element_tile,
-        node.reshape(NBLK, SEG), base.reshape(3, NBLK, SEG), contact_bin.reshape(-1),
-    )
+        in_specs=[vmem] * 3,
+        out_specs=(hbm, hbm, hbm),
+        scratch_shapes=[dma((2 * ZT + 1,))],
+        name="deliver",
+    )(*[pltpu.with_memory_space_constraint(x, pltpu.VMEM) for x in results])
     return new_displacement, new_velocity, heat.reshape(-1)
 
 

time: 94.9 us -> 74.7 us (0.79)
  Pallas kernels: 86.7 us -> 73.4 us
  local copies, waits for them, and re-layouts: 6.2 us -> 0 us
    pallas_call x1 -> x2, Pallas kernels: 86.7 us -> 73.4 us  [the longest x1 72.2 us: per_device(): pl.pallas_call(kernel, out_shape=(pltpu.VMEM((3, CX) + slab, F32), pltpu....]
    unnamed x11 -> x0, local copies, waits for them, and re-layouts: 5.6 us -> none
where the time goes in v2:
time: 74.7 us; the launch traced here: 74 us
  Pallas kernels  73.4 us (98%)
    pallas_call x1, Pallas kernels, per_device(): pl.pallas_call(kernel, out_shape=(pltpu.VMEM((3, CX) + slab, F32), pltpu....  72.2 us

profile of v2, /device:TPU:39, one launch (start us, length us, event | category | flops | bytes accessed | tf_op | source)
XLA Modules:
  0.0 74.0 jit_solution(10399962773987900927)
XLA Ops:
  0.6 72.2 %module_substeps.1 = (f32[3,8,4,16,128]{4,3,2,1,0:T(8,128)S(1)}, f32[3,8,4,16,128]{4,3,2,1,0:T(8,128)S(1)}, f32[2,128]{1,0:T(2,128)S(1)}) custom-call(f32[3,8,16,512]{3,2,1,0:T(8,128)} %disp_in.1, f32[3,8,16,512]{3,2,1,0:T(8,128)} %velo_in.1, f32[2,8,16,512]{3,2,1,0:T(8,128)} %moduli_in.1, f32[8,16,512]{2,1,0:T(8,128)} %mass_in.1, s32[8,16,512]{2,1,0:T(8,128)} %tile_in.1, ...), custom_call_target="tpu_custom_call" | custom-call | tf_op jit(solution)/shard_map/module_substeps/pallas_call | solution.py:528
  72.8 1.2 %deliver.1 = (f32[3,8,16,512]{3,2,1,0:T(8,128)}, f32[3,8,16,512]{3,2,1,0:T(8,128)}, f32[2,128]{1,0:T(2,128)}) custom-call(f32[3,8,4,16,128]{4,3,2,1,0:T(8,128)S(1)} %get-tuple-element.9.disp, f32[3,8,4,16,128]{4,3,2,1,0:T(8,128)S(1)} %get-tuple-element.10.velo, f32[2,128]{1,0:T(2,128)S(1)} %get-tuple-element.11.heat), custom_call_target="tpu_custom_call" | custom-call | tf_op jit(solution)/shard_map/deliver/pallas_call | solution.py:546

commit v3 on v2

--- a/solution.py
+++ b/solution.py
@@ -20,8 +20,10 @@
 NSEG = NBLK * SEG
 ROWS = CX * ZT * CY
 PIECES = 2
+ROWS_OWN, ROWS_OVER, ROWS_NEXT = 64, 64, 64
 WIDE = 384
 FAR = 1e12
+NEXT, OVER, EMPTY = NBIN * CAP, 2 * NBIN * CAP, 3 * NBIN * CAP
 MESH = pl.DeviceIdType.MESH
 F32, BF16, I32 = jnp.float32, jnp.bfloat16, jnp.int32
 
@@ -61,13 +63,15 @@
     disp, moduli, inverse, tiles,
     one_seg, one_node, lane_col, base_col, tile_lane, tile_row,
     split_disp, split_push, seg_col, seg_row, outgoing, pool, spread,
+    met_own, met_next, met_over, own_rows, return_out, return_in, heat_row,
     push_acc, heat_acc, picked, pushed,
     grads, stress, near, far,
     col_out, col_in, corner_out, corner_in,
     layer_force_out, layer_force_in, col_force_out, col_force_in,
     corner_force_out, corner_force_in,
-    heat_parts, heat_in, slots,
-    in_sem, send_sem, recv_sem, point_send, point_recv, heat_send, heat_recv,
+    heat_parts, heat_in, slots, ranks,
+    in_sem, send_sem, recv_sem, point_send, point_recv, return_send, return_recv,
+    heat_send, heat_recv,
 ):
     dom, own = lax.axis_index("dom"), lax.axis_index("bin")
     doms, bins = lax.axis_size("dom"), lax.axis_size("bin")
@@ -99,7 +103,12 @@
         stress[k, CX + 1] = jnp.zeros((ZT, CY, 128), F32)
     for p in range(3):
         far[p, CX, :, 0:8, :] = jnp.zeros((ZT, 8, 128), F32)
-        seg_row[NBLK] = jnp.full((4, 128), FAR, F32)
+        spread[EMPTY, p] = jnp.full((8, 128), FAR, F32)
+    seg_row[NBLK] = jnp.full((4, 128), FAR, F32)
+    met_own[NBLK] = jnp.zeros((2, 4, 8, 128), F32)
+    met_next[NBLK] = jnp.zeros((4, 4, 8, 128), F32)
+    met_over[NBLK] = jnp.zeros((2, 4, 8, 128), F32)
+    heat_row[...] = jnp.zeros_like(heat_row)
 
     barrier = pltpu.get_barrier_semaphore()
     peers = [(dom, lax.rem(own + i, bins), None) for i in range(1, NBIN)]
@@ -115,6 +124,11 @@
 
     def fill_slots(step, carry):
         named = [bins_ref[step, 0, b] for b in range(NBLK)]
+        for b in range(NBLK):
+            rank = jnp.int32(0)
+            for before in range(b):
+                rank = rank + (named[before] == named[b]).astype(I32)
+            ranks[step * NBLK + b] = rank
         for k in range(NBIN):
             count = jnp.int32(0)
             found = [jnp.int32(NBLK)] * CAP
@@ -185,37 +199,67 @@
     col_force_copy = remote(col_force_out, col_force_in, 4, dom, own + 1)
     corner_force_copy = remote(corner_force_out, corner_force_in, 5, dom + 1, own + 1)
 
-    def touching(ahead, step, fresh):
-        def rows_of(i, carry):
-            at = pl.ds(pl.multiple_of(i * 16, 16), 16)
-            mine = [seg_col[c, at, :].reshape(2, 8, 128) for c in range(3)]
-            named = bins_ref[step, 0, i // 8]
-            sums = [
-                jnp.zeros((2, 8, 128), F32) if fresh else push_acc[c, at, :].reshape(2, 8, 128)
-                for c in range(3)
-            ]
-            heat = heat_acc[at, :].reshape(2, 8, 128)
-            for i in ahead:
-                for k in range(CAP):
-                    slot = i * (NBIN * CAP) + named * CAP + k
+    def touching(step, slots_of, met, rows, itself):
+        def with_block(b, carry):
+            facing = slots_of(bins_ref[step, 0, b], ranks[step * NBLK + b])
+
+            def with_rows(g, met_sums):
+                met_sums = [list(each) for each in met_sums]
+                at = pl.ds(pl.multiple_of(b * SEG + g * rows, rows), rows)
+                wide = (rows // 8, 8, 128)
+                mine = [seg_col[c, at, :].reshape(wide) for c in range(3)]
+                if itself:
+                    sums = [jnp.zeros(wide, F32) for c in range(3)]
+                else:
+                    sums = [push_acc[c, at, :].reshape(wide) for c in range(3)]
+                heat = heat_acc[at, :].reshape(wide)
+                for j, slot in enumerate(facing):
                     delta = [mine[c] - spread[slot, c] for c in range(3)]
                     square = delta[0] * delta[0] + delta[1] * delta[1] + delta[2] * delta[2]
                     square = jnp.maximum(square, 1e-30)
                     over = lax.rsqrt(square)
                     pressure = jnp.maximum(RADIUS - square * over, 0.0)
                     weight = pressure * jnp.minimum(over, 1.0 / (0.25 * RADIUS))
-                    heat = heat + pressure * pressure
-                    sums = [sums[c] + weight * delta[c] for c in range(3)]
-            for c in range(3):
-                push_acc[c, at, :] = sums[c].reshape(16, 128)
-            heat_acc[at, :] = heat.reshape(16, 128)
-            return carry
-
-        lax.fori_loop(0, NSEG // 16, rows_of, 0)
+                    parts = [weight * delta[c] for c in range(3)] + [pressure * pressure]
+                    sums = [sums[c] + parts[c] for c in range(3)]
+                    heat = heat + parts[3]
+                    if itself and j == 0:
+                        continue
+                    row = met_sums[j - itself]
+                    for q in range(4):
+                        row[q] = row[q] + jnp.sum(parts[q], axis=0)
+                for c in range(3):
+                    push_acc[c, at, :] = sums[c].reshape(rows, 128)
+                heat_acc[at, :] = heat.reshape(rows, 128)
+                return met_sums
+
+            none = [[jnp.zeros((8, 128), F32)] * 4 for _ in facing[itself:]]
+            met_sums = lax.fori_loop(0, SEG // rows, with_rows, none)
+            for j, each in enumerate(met_sums):
+                for q in range(4):
+                    met[b, j, q] = each[q]
+            return carry
+
+        lax.fori_loop(0, NBLK, with_block, 0)
+
+    high = (own >= NBIN // 2).astype(I32)
+
+    def own_slots(named, rank):
+        base = named * CAP
+        opposite = jnp.where(rank < CAP // 2, base + ((rank + 2) & (CAP - 1)), EMPTY)
+        return [base + rank, base + ((rank + 1) & (CAP - 1)), opposite]
+
+    def next_slots(named, rank):
+        return [NEXT + named * CAP + k for k in range(CAP)]
+
+    def over_slots(named, rank):
+        first = OVER + named * CAP + ((rank + high) & 1)
+        return [first, first + 2]
+
+    def rows_of(values):
+        return jnp.sum(functools.reduce(lambda a, b: a + b, values), axis=0, keepdims=True)
 
     def substep(step, carry):
-        parity = lax.rem(step, 2)
-
         for c in range(3):
             for z in range(ZT):
                 corner_out[c * ZT + z : c * ZT + z + 1, :] = disp[c, 0, z, 8:9, :]
@@ -258,10 +302,22 @@
             outgoing[slot] = block
             for c in range(3):
                 spread[slot, c] = jnp.broadcast_to(block[c : c + 1, :], (8, 128))
-        for i in range(1, NBIN):
-            point_copy(i, parity).start()
-
-        touching([0], step, True)
+        for i in range(2):
+            point_copy(i).start()
+
+        touching(step, own_slots, met_own, ROWS_OWN, 1)
+
+        def gather_own(k, carry):
+            named = [slots[step * (NBIN * CAP) + k * CAP + r] for r in range(CAP)]
+            for r in range(CAP):
+                for q in range(4):
+                    values = [met_own[named[(r + 3) % CAP], 0, q]]
+                    if r >= CAP // 2:
+                        values.append(met_own[named[r - CAP // 2], 1, q])
+                    own_rows[k * CAP + r, q : q + 1, :] = rows_of(values)
+            return carry
+
+        lax.fori_loop(0, NBIN, gather_own, 0)
 
         pl.when(dom_up)(layer_copy.wait_recv)
         pl.when(bin_up)(col_copy.wait_recv)
@@ -302,6 +358,47 @@
 
         lax.fori_loop(0, CX, stresses, 0)
 
+        def spread_from(i):
+            point_copy(i).wait_recv()
+
+            def spread_slot(slot, carry):
+                block = pool[i, slot]
+                for c in range(3):
+                    spread[NEXT * (i + 1) + slot, c] = jnp.broadcast_to(
+                        block[c : c + 1, :], (8, 128)
+                    )
+                return carry
+
+            lax.fori_loop(0, NBIN * CAP, spread_slot, 0)
+
+        spread_from(1)
+        touching(step, over_slots, met_over, ROWS_OVER, 0)
+
+        def gather_over(k, carry):
+            for r in range(CAP):
+                first = step * (NBIN * CAP) + k * CAP + ((r + high) & 1)
+                named = [slots[first], slots[first + 2]]
+                for q in range(4):
+                    values = [met_over[each, r // 2, q] for each in named]
+                    return_out[1, k * CAP + r, q : q + 1, :] = rows_of(values)
+            return carry
+
+        lax.fori_loop(0, NBIN, gather_over, 0)
+        return_copy(1).start()
+        spread_from(0)
+        touching(step, next_slots, met_next, ROWS_NEXT, 0)
+
+        def gather_next(k, carry):
+            named = [slots[step * (NBIN * CAP) + k * CAP + r] for r in range(CAP)]
+            for r in range(CAP):
+                for q in range(4):
+                    values = [met_next[each, r, q] for each in named]
+                    return_out[0, k * CAP + r, q : q + 1, :] = rows_of(values)
+            return carry
+
+        lax.fori_loop(0, NBIN, gather_next, 0)
+        return_copy(0).start()
+
         def forces(part, carry):
             for x in [3 * part + i for i in range(3)]:
                 for p, (kx, ky, kz) in enumerate(((0, 3, 4), (3, 1, 5), (4, 5, 2))):
@@ -324,27 +421,19 @@
         pl.when(bin_up)(col_force_copy.start)
         pl.when(diag_up)(corner_force_copy.start)
 
-        for i in range(1, NBIN):
-            point_copy(i, parity).wait_recv()
-
-        def spread_slot(slot, carry):
-            for i in range(1, NBIN):
-                block = pool[parity, lax.rem(own + i, bins), slot]
-                for c in range(3):
-                    spread[i * (NBIN * CAP) + slot, c] = jnp.broadcast_to(
-                        block[c : c + 1, :], (8, 128)
-                    )
-            return carry
-
-        lax.fori_loop(0, NBIN * CAP, spread_slot, 0)
-        touching(range(1, NBIN), step, False)
+        for i in range(2):
+            return_copy(i).wait_recv()
 
         def lay_push(pair, carry):
             for b in (2 * pair, 2 * pair + 1):
                 at = pl.ds(pl.multiple_of(b * SEG, SEG), SEG)
                 mask = lane_col[at, :] == lanes_of((SEG, SEG)).astype(F32)
+                slot = bins_ref[step, 0, b] * CAP + ranks[step * NBLK + b]
+                met = own_rows[slot] + return_in[0, slot] + return_in[1, slot]
+                heat_row[b] = heat_row[b] + met[3:4, :]
                 for c in range(3):
-                    total = jnp.sum(push_acc[c, at, :], axis=1, keepdims=True)
+                    total = push_acc[c, at, :] - jnp.where(eye, met[c : c + 1, :], 0.0)
+                    total = jnp.sum(total, axis=1, keepdims=True)
                     laid = jnp.where(mask, PENALTY * total, 0.0)
                     for p, part in enumerate(pieces_of(laid)):
                         split_push[at, p * WIDE + c * 128 : p * WIDE + c * 128 + 128] = part
@@ -370,8 +459,9 @@
         pl.when(dom_up)(layer_force_copy.wait_send)
         pl.when(bin_up)(col_force_copy.wait_send)
         pl.when(diag_up)(corner_force_copy.wait_send)
-        for i in range(1, NBIN):
-            point_copy(i, parity).wait_send()
+        for i in range(2):
+            point_copy(i).wait_send()
+            return_copy(i).wait_send()
 
         def advance(x, carry):
             for p in range(3):
@@ -390,11 +480,18 @@
         lax.fori_loop(0, CX, advance, 0)
         return carry
 
-    def point_copy(i, parity):
+    def point_copy(i):
         return pltpu.make_async_remote_copy(
-            src_ref=outgoing, dst_ref=pool.at[parity, own],
-            send_sem=point_send.at[i - 1], recv_sem=point_recv.at[parity, i - 1],
-            device_id=(dom, lax.rem(own + i, bins)), device_id_type=MESH,
+            src_ref=outgoing, dst_ref=pool.at[i],
+            send_sem=point_send.at[i], recv_sem=point_recv.at[i],
+            device_id=(dom, lax.rem(own + bins - 1 - i, bins)), device_id_type=MESH,
+        )
+
+    def return_copy(i):
+        return pltpu.make_async_remote_copy(
+            src_ref=return_out.at[i], dst_ref=return_in.at[i],
+            send_sem=return_send.at[i], recv_sem=return_recv.at[i],
+            device_id=(dom, lax.rem(own + 1 + i, bins)), device_id_type=MESH,
         )
 
     lax.fori_loop(0, SUB, substep, 0)
@@ -423,7 +520,8 @@
         row_col = jnp.sum(jnp.where(mask, picked[:, 0:128], 0.0), axis=1, keepdims=True)
         lane = jnp.sum(jnp.where(mask, picked[:, 128:256], 0.0), axis=1, keepdims=True)
         tile_row[b, 0:1, :] = jnp.sum(jnp.where(eye, row_col, 0.0), axis=0, keepdims=True)
-        total = SHORT_GAIN * jnp.sum(heat_acc[at, :], axis=1, keepdims=True)
+        total = heat_acc[at, :] + jnp.where(eye, heat_row[b], 0.0)
+        total = SHORT_GAIN * jnp.sum(total, axis=1, keepdims=True)
         laid = jnp.where(lane == ids, total, 0.0)
         for p, part in enumerate(pieces_of(laid)):
             tile_lane[p, at, :] = part
@@ -494,8 +592,15 @@
         vec((3, NSEG, 128), F32),
         vec((NBLK + 1, 4, 128), F32),
         vec((NBIN * CAP, 4, 128), F32),
-        vec((2, NBIN, NBIN * CAP, 4, 128), F32),
-        vec((NBIN * NBIN * CAP, 3, 8, 128), F32),
+        vec((2, NBIN * CAP, 4, 128), F32),
+        vec((3 * NBIN * CAP + 1, 3, 8, 128), F32),
+        vec((NBLK + 1, 2, 4, 8, 128), F32),
+        vec((NBLK + 1, 4, 4, 8, 128), F32),
+        vec((NBLK + 1, 2, 4, 8, 128), F32),
+        vec((NBIN * CAP, 4, 128), F32),
+        vec((2, NBIN * CAP, 4, 128), F32),
+        vec((2, NBIN * CAP, 4, 128), F32),
+        vec((NBLK, 1, 128), F32),
         vec((3, NSEG, 128), F32),
         vec((NSEG, 128), F32),
         vec((NSEG, PIECES * WIDE), F32),
@@ -517,11 +622,14 @@
         vec((3, 8, 128), F32),
         vec((2, 8, 128), F32),
         pltpu.SMEM((SUB * NBIN * CAP,), I32),
+        pltpu.SMEM((SUB * NBLK,), I32),
         dma((5 * ZT,)),
         dma((6,)),
         dma((6,)),
-        dma((NBIN - 1,)),
-        dma((2, NBIN - 1)),
+        dma((2,)),
+        dma((2,)),
+        dma((2,)),
+        dma((2,)),
         dma((2,)),
         dma((2,)),
     ]

time: 74.7 us -> 75.9 us (1.016)
  Pallas kernels: 73.4 us -> 75.1 us
    pallas_call x1, Pallas kernels: 72.2 us -> 73.9 us  [per_device(): pl.pallas_call(kernel, out_shape=(pltpu.VMEM((3, CX) + slab, F32), pltpu....]
where the time goes in v3:
time: 75.9 us; the launch traced here: 75.8 us
  Pallas kernels  75.1 us (99%)
    pallas_call x1, Pallas kernels, per_device(): pl.pallas_call(kernel, out_shape=(pltpu.VMEM((3, CX) + slab, F32), pltpu....  73.9 us

profile of v3, /device:TPU:39, one launch (start us, length us, event | category | flops | bytes accessed | tf_op | source)
XLA Modules:
  0.0 75.8 jit_solution(12704412088030364017)
XLA Ops:
  0.6 73.9 %module_substeps.1 = (f32[3,8,4,16,128]{4,3,2,1,0:T(8,128)S(1)}, f32[3,8,4,16,128]{4,3,2,1,0:T(8,128)S(1)}, f32[2,128]{1,0:T(2,128)S(1)}) custom-call(f32[3,8,16,512]{3,2,1,0:T(8,128)} %disp_in.1, f32[3,8,16,512]{3,2,1,0:T(8,128)} %velo_in.1, f32[2,8,16,512]{3,2,1,0:T(8,128)} %moduli_in.1, f32[8,16,512]{2,1,0:T(8,128)} %mass_in.1, s32[8,16,512]{2,1,0:T(8,128)} %tile_in.1, ...), custom_call_target="tpu_custom_call" | custom-call | tf_op jit(solution)/shard_map/module_substeps/pallas_call | solution.py:636
  74.5 1.2 %deliver.1 = (f32[3,8,16,512]{3,2,1,0:T(8,128)}, f32[3,8,16,512]{3,2,1,0:T(8,128)}, f32[2,128]{1,0:T(2,128)}) custom-call(f32[3,8,4,16,128]{4,3,2,1,0:T(8,128)S(1)} %get-tuple-element.9.disp, f32[3,8,4,16,128]{4,3,2,1,0:T(8,128)S(1)} %get-tuple-element.10.velo, f32[2,128]{1,0:T(2,128)S(1)} %get-tuple-element.11.heat), custom_call_target="tpu_custom_call" | custom-call | tf_op jit(solution)/shard_map/deliver/pallas_call | solution.py:654

commit v4 on v2

--- a/solution.py
+++ b/solution.py
@@ -20,8 +20,13 @@
 NSEG = NBLK * SEG
 ROWS = CX * ZT * CY
 PIECES = 2
+ROWS_OWN, ROWS_OVER, ROWS_NEXT = 64, 64, 64
 WIDE = 384
 FAR = 1e12
+BINS = SUB * NBIN * CAP
+RANKS = BINS + SUB * NBLK
+TABLE = RANKS + SUB * NBLK
+NEXT, OVER, LAST = NBLK + 1, 2 * (NBLK + 1), 3 * (NBLK + 1)
 MESH = pl.DeviceIdType.MESH
 F32, BF16, I32 = jnp.float32, jnp.bfloat16, jnp.int32
 
@@ -60,14 +65,16 @@
     disp_out, velo, heat_out,
     disp, moduli, inverse, tiles,
     one_seg, one_node, lane_col, base_col, tile_lane, tile_row,
-    split_disp, split_push, seg_col, seg_row, outgoing, pool, spread,
+    split_disp, split_push, seg_col, seg_row, pool, spread,
+    met_own, met_over, own_rows, return_out, return_in, heat_row,
     push_acc, heat_acc, picked, pushed,
     grads, stress, near, far,
     col_out, col_in, corner_out, corner_in,
     layer_force_out, layer_force_in, col_force_out, col_force_in,
     corner_force_out, corner_force_in,
-    heat_parts, heat_in, slots,
-    in_sem, send_sem, recv_sem, point_send, point_recv, heat_send, heat_recv,
+    heat_parts, heat_in, table, tables,
+    in_sem, send_sem, recv_sem, point_send, point_recv, return_send, return_recv,
+    heat_send, heat_recv, table_send, table_recv,
 ):
     dom, own = lax.axis_index("dom"), lax.axis_index("bin")
     doms, bins = lax.axis_size("dom"), lax.axis_size("bin")
@@ -99,7 +106,11 @@
         stress[k, CX + 1] = jnp.zeros((ZT, CY, 128), F32)
     for p in range(3):
         far[p, CX, :, 0:8, :] = jnp.zeros((ZT, 8, 128), F32)
-        seg_row[NBLK] = jnp.full((4, 128), FAR, F32)
+        for i in range(NBIN):
+            spread[i * (NBLK + 1) + NBLK, p] = jnp.full((8, 128), FAR, F32)
+    met_own[NBLK] = jnp.zeros((2, 4, 8, 128), F32)
+    met_over[NBLK] = jnp.zeros((2, 4, 8, 128), F32)
+    heat_row[...] = jnp.zeros_like(heat_row)
 
     barrier = pltpu.get_barrier_semaphore()
     peers = [(dom, lax.rem(own + i, bins), None) for i in range(1, NBIN)]
@@ -115,6 +126,12 @@
 
     def fill_slots(step, carry):
         named = [bins_ref[step, 0, b] for b in range(NBLK)]
+        for b in range(NBLK):
+            rank = jnp.int32(0)
+            for before in range(b):
+                rank = rank + (named[before] == named[b]).astype(I32)
+            table[RANKS + step * NBLK + b] = rank & (CAP - 1)
+            table[BINS + step * NBLK + b] = named[b]
         for k in range(NBIN):
             count = jnp.int32(0)
             found = [jnp.int32(NBLK)] * CAP
@@ -126,7 +143,7 @@
                     )
                 count = count + same.astype(I32)
             for rank in range(CAP):
-                slots[(step * NBIN + k) * CAP + rank] = found[rank]
+                table[(step * NBIN + k) * CAP + rank] = found[rank]
         return carry
 
     lax.fori_loop(0, SUB, fill_slots, 0)
@@ -177,6 +194,15 @@
             device_id=(to_dom, to_bin), device_id_type=MESH,
         )
 
+    def table_copy(i):
+        return pltpu.make_async_remote_copy(
+            src_ref=table, dst_ref=tables.at[i],
+            send_sem=table_send.at[i], recv_sem=table_recv.at[i],
+            device_id=(dom, lax.rem(own + bins - 1 - i, bins)), device_id_type=MESH,
+        )
+
+    for i in range(NBIN - 1):
+        table_copy(i).start()
     inner = pl.ds(8, CY)
     layer_copy = remote(disp.at[:, 0, :, inner, :], disp.at[:, CX, :, inner, :], 0, dom - 1, own)
     col_copy = remote(col_out, col_in, 1, dom, own - 1)
@@ -185,33 +211,71 @@
     col_force_copy = remote(col_force_out, col_force_in, 4, dom, own + 1)
     corner_force_copy = remote(corner_force_out, corner_force_in, 5, dom + 1, own + 1)
 
-    def touching(ahead, step, fresh):
-        def rows_of(i, carry):
-            at = pl.ds(pl.multiple_of(i * 16, 16), 16)
-            mine = [seg_col[c, at, :].reshape(2, 8, 128) for c in range(3)]
-            named = bins_ref[step, 0, i // 8]
-            sums = [
-                jnp.zeros((2, 8, 128), F32) if fresh else push_acc[c, at, :].reshape(2, 8, 128)
-                for c in range(3)
-            ]
-            heat = heat_acc[at, :].reshape(2, 8, 128)
-            for i in ahead:
-                for k in range(CAP):
-                    slot = i * (NBIN * CAP) + named * CAP + k
+    def touching(step, slots_of, met, rows, alone):
+        def with_block(b, carry):
+            facing = slots_of(step, *mine_of(table, step, b))
+
+            def with_rows(g, met_sums):
+                met_sums = [list(each) for each in met_sums]
+                at = pl.ds(pl.multiple_of(b * SEG + g * rows, rows), rows)
+                wide = (rows // 8, 8, 128)
+                mine = [seg_col[c, at, :].reshape(wide) for c in range(3)]
+                if met is met_own:
+                    sums = [jnp.zeros(wide, F32) for c in range(3)]
+                else:
+                    sums = [push_acc[c, at, :].reshape(wide) for c in range(3)]
+                heat = heat_acc[at, :].reshape(wide)
+                for j, slot in enumerate(facing):
                     delta = [mine[c] - spread[slot, c] for c in range(3)]
                     square = delta[0] * delta[0] + delta[1] * delta[1] + delta[2] * delta[2]
                     square = jnp.maximum(square, 1e-30)
                     over = lax.rsqrt(square)
                     pressure = jnp.maximum(RADIUS - square * over, 0.0)
                     weight = pressure * jnp.minimum(over, 1.0 / (0.25 * RADIUS))
-                    heat = heat + pressure * pressure
-                    sums = [sums[c] + weight * delta[c] for c in range(3)]
-            for c in range(3):
-                push_acc[c, at, :] = sums[c].reshape(16, 128)
-            heat_acc[at, :] = heat.reshape(16, 128)
-            return carry
-
-        lax.fori_loop(0, NSEG // 16, rows_of, 0)
+                    parts = [weight * delta[c] for c in range(3)] + [pressure * pressure]
+                    sums = [sums[c] + parts[c] for c in range(3)]
+                    heat = heat + parts[3]
+                    if j < alone:
+                        continue
+                    row = met_sums[j - alone]
+                    for q in range(4):
+                        row[q] = row[q] + jnp.sum(parts[q], axis=0)
+                for c in range(3):
+                    push_acc[c, at, :] = sums[c].reshape(rows, 128)
+                heat_acc[at, :] = heat.reshape(rows, 128)
+                return met_sums
+
+            none = [[jnp.zeros((8, 128), F32)] * 4 for _ in facing[alone:]]
+            met_sums = lax.fori_loop(0, SEG // rows, with_rows, none)
+            for j, each in enumerate(met_sums):
+                for q in range(4):
+                    met[b, j, q] = each[q]
+            return carry
+
+        lax.fori_loop(0, NBLK, with_block, 0)
+
+    high = (own >= NBIN // 2).astype(I32)
+
+    def mine_of(numbers, step, b):
+        return numbers[BINS + step * NBLK + b], numbers[RANKS + step * NBLK + b]
+
+    def own_slots(step, named, rank):
+        base = step * (NBIN * CAP) + named * CAP
+        opposite = table[base + ((rank + 2) & (CAP - 1))]
+        opposite = jnp.where(rank < CAP // 2, opposite, NBLK)
+        return [table[base + rank], table[base + ((rank + 1) & (CAP - 1))], opposite]
+
+    def next_slots(step, named, rank):
+        base = step * (NBIN * CAP) + named * CAP
+        ahead = [NEXT + tables[0, base + k] for k in range(CAP)]
+        return ahead + [LAST + tables[2, base + k] for k in range(CAP)]
+
+    def over_slots(step, named, rank):
+        first = step * (NBIN * CAP) + named * CAP + ((rank + high) & 1)
+        return [OVER + tables[1, first], OVER + tables[1, first + 2]]
+
+    def rows_of(values):
+        return jnp.sum(functools.reduce(lambda a, b: a + b, values), axis=0, keepdims=True)
 
     def substep(step, carry):
         parity = lax.rem(step, 2)
@@ -247,21 +311,29 @@
                     moved = jnp.where(mask, value, 0.0)
                     column = base_col[c, at, :] + jnp.sum(moved, axis=1, keepdims=True)
                     seg_col[c, at, :] = column
-                    seg_row[b, c : c + 1, :] = jnp.sum(
-                        jnp.where(eye, column, 0.0), axis=0, keepdims=True
-                    )
+                    row = jnp.sum(jnp.where(eye, column, 0.0), axis=0, keepdims=True)
+                    seg_row[c, pl.ds(b, 1), :] = row
+                    spread[b, c] = jnp.broadcast_to(row, (8, 128))
             return carry
 
         lax.fori_loop(0, NBLK // 2, positions, 0)
-        for slot in range(NBIN * CAP):
-            block = seg_row[slots[step * (NBIN * CAP) + slot]]
-            outgoing[slot] = block
-            for c in range(3):
-                spread[slot, c] = jnp.broadcast_to(block[c : c + 1, :], (8, 128))
-        for i in range(1, NBIN):
+        for i in range(NBIN - 1):
             point_copy(i, parity).start()
 
-        touching([0], step, True)
+        touching(step, own_slots, met_own, ROWS_OWN, 1)
+
+        def gather_own(b, carry):
+            named, rank = mine_of(table, step, b)
+            base = step * (NBIN * CAP) + named * CAP
+            beside = table[base + ((rank + 3) & (CAP - 1))]
+            opposite = table[base + ((rank + 2) & (CAP - 1))]
+            opposite = jnp.where(rank >= CAP // 2, opposite, NBLK)
+            for q in range(4):
+                row = rows_of([met_own[beside, 0, q], met_own[opposite, 1, q]])
+                own_rows[b, q : q + 1, :] = row
+            return carry
+
+        lax.fori_loop(0, NBLK, gather_own, 0)
 
         pl.when(dom_up)(layer_copy.wait_recv)
         pl.when(bin_up)(col_copy.wait_recv)
@@ -302,49 +374,78 @@
 
         lax.fori_loop(0, CX, stresses, 0)
 
-        def forces(part, carry):
-            for x in [3 * part + i for i in range(3)]:
-                for p, (kx, ky, kz) in enumerate(((0, 3, 4), (3, 1, 5), (4, 5, 2))):
-                    along_x = stress[kx, x] - stress[kx, x + 1]
-                    along_y = stress[ky, x] + stress[ky, x + 1]
-                    along_z = stress[kz, x] + stress[kz, x + 1]
-                    minus, plus = along_x - along_y, along_x + along_y
-                    near[p, x] = (minus - along_z) + last_z(minus + along_z)
-                    far[p, x, :, 8:24, :] = (plus - along_z) + last_z(plus + along_z)
-            return carry
-
-        lax.fori_loop(0, (CX + 1) // 3, forces, 0)
+        def forces_on(x):
+            for p, (kx, ky, kz) in enumerate(((0, 3, 4), (3, 1, 5), (4, 5, 2))):
+                along_x = stress[kx, x] - stress[kx, x + 1]
+                along_y = stress[ky, x] + stress[ky, x + 1]
+                along_z = stress[kz, x] + stress[kz, x + 1]
+                minus, plus = along_x - along_y, along_x + along_y
+                near[p, x] = (minus - along_z) + last_z(minus + along_z)
+                far[p, x, :, 8:24, :] = (plus - along_z) + last_z(plus + along_z)
+
+        forces_on(CX)
         for p in range(3):
             layer_force_out[p] = near[p, CX] + far[p, CX, :, 7:23, :]
             for z in range(ZT):
                 corner_force_out[p * ZT + z : p * ZT + z + 1, :] = far[p, CX, z, 23:24, :]
+        pl.when(dom_up)(layer_force_copy.start)
+        pl.when(diag_up)(corner_force_copy.start)
+
+        def forces(pair, carry):
+            for x in (2 * pair, 2 * pair + 1):
+                forces_on(x)
+            return carry
+
+        lax.fori_loop(0, CX // 2, forces, 0)
+        for p in range(3):
+            for z in range(ZT):
                 for x in range(CX):
                     col_force_out[p, z, x : x + 1, :] = far[p, x, z, 23:24, :]
-        pl.when(dom_up)(layer_force_copy.start)
         pl.when(bin_up)(col_force_copy.start)
-        pl.when(diag_up)(corner_force_copy.start)
-
-        for i in range(1, NBIN):
+
+        @pl.when(step == 0)
+        def tables_here():
+            for i in range(NBIN - 1):
+                table_copy(i).wait()
+
+        def spread_from(i):
             point_copy(i, parity).wait_recv()
-
-        def spread_slot(slot, carry):
-            for i in range(1, NBIN):
-                block = pool[parity, lax.rem(own + i, bins), slot]
+            for b in range(NBLK):
                 for c in range(3):
-                    spread[i * (NBIN * CAP) + slot, c] = jnp.broadcast_to(
-                        block[c : c + 1, :], (8, 128)
+                    spread[NEXT * (i + 1) + b, c] = jnp.broadcast_to(
+                        pool[parity, i, c, b : b + 1, :], (8, 128)
                     )
-            return carry
-
-        lax.fori_loop(0, NBIN * CAP, spread_slot, 0)
-        touching(range(1, NBIN), step, False)
+
+        spread_from(1)
+        touching(step, over_slots, met_over, ROWS_OVER, 0)
+
+        def gather_over(b, carry):
+            named, rank = mine_of(tables.at[1], step, b)
+            first = step * (NBIN * CAP) + named * CAP + ((rank + high) & 1)
+            ones = [table[first], table[first + 2]]
+            half = lax.shift_right_logical(rank, 1)
+            for q in range(4):
+                row = rows_of([met_over[one, half, q] for one in ones])
+                return_out[b, q : q + 1, :] = row
+            return carry
+
+        lax.fori_loop(0, NBLK, gather_over, 0)
+        return_copy.start()
+        spread_from(0)
+        spread_from(2)
+        touching(step, next_slots, None, ROWS_NEXT, 2 * CAP)
+
+        return_copy.wait_recv()
 
         def lay_push(pair, carry):
             for b in (2 * pair, 2 * pair + 1):
                 at = pl.ds(pl.multiple_of(b * SEG, SEG), SEG)
                 mask = lane_col[at, :] == lanes_of((SEG, SEG)).astype(F32)
+                met = own_rows[b] + return_in[b]
+                heat_row[b] = heat_row[b] + met[3:4, :]
                 for c in range(3):
-                    total = jnp.sum(push_acc[c, at, :], axis=1, keepdims=True)
+                    total = push_acc[c, at, :] - jnp.where(eye, met[c : c + 1, :], 0.0)
+                    total = jnp.sum(total, axis=1, keepdims=True)
                     laid = jnp.where(mask, PENALTY * total, 0.0)
                     for p, part in enumerate(pieces_of(laid)):
                         split_push[at, p * WIDE + c * 128 : p * WIDE + c * 128 + 128] = part
@@ -370,8 +471,9 @@
         pl.when(dom_up)(layer_force_copy.wait_send)
         pl.when(bin_up)(col_force_copy.wait_send)
         pl.when(diag_up)(corner_force_copy.wait_send)
-        for i in range(1, NBIN):
+        for i in range(NBIN - 1):
             point_copy(i, parity).wait_send()
+        return_copy.wait_send()
 
         def advance(x, carry):
             for p in range(3):
@@ -392,10 +494,15 @@
 
     def point_copy(i, parity):
         return pltpu.make_async_remote_copy(
-            src_ref=outgoing, dst_ref=pool.at[parity, own],
-            send_sem=point_send.at[i - 1], recv_sem=point_recv.at[parity, i - 1],
-            device_id=(dom, lax.rem(own + i, bins)), device_id_type=MESH,
+            src_ref=seg_row, dst_ref=pool.at[parity, i],
+            send_sem=point_send.at[i], recv_sem=point_recv.at[parity, i],
+            device_id=(dom, lax.rem(own + bins - 1 - i, bins)), device_id_type=MESH,
         )
+
+    return_copy = pltpu.make_async_remote_copy(
+        src_ref=return_out, dst_ref=return_in, send_sem=return_send.at[0],
+        recv_sem=return_recv.at[0], device_id=(dom, lax.rem(own + 2, bins)), device_id_type=MESH,
+    )
 
     lax.fori_loop(0, SUB, substep, 0)
 
@@ -423,7 +530,8 @@
         row_col = jnp.sum(jnp.where(mask, picked[:, 0:128], 0.0), axis=1, keepdims=True)
         lane = jnp.sum(jnp.where(mask, picked[:, 128:256], 0.0), axis=1, keepdims=True)
         tile_row[b, 0:1, :] = jnp.sum(jnp.where(eye, row_col, 0.0), axis=0, keepdims=True)
-        total = SHORT_GAIN * jnp.sum(heat_acc[at, :], axis=1, keepdims=True)
+        total = heat_acc[at, :] + jnp.where(eye, heat_row[b], 0.0)
+        total = SHORT_GAIN * jnp.sum(total, axis=1, keepdims=True)
         laid = jnp.where(lane == ids, total, 0.0)
         for p, part in enumerate(pieces_of(laid)):
             tile_lane[p, at, :] = part
@@ -492,10 +600,15 @@
         vec((ROWS, PIECES * WIDE), BF16),
         vec((NSEG, PIECES * WIDE), BF16),
         vec((3, NSEG, 128), F32),
-        vec((NBLK + 1, 4, 128), F32),
-        vec((NBIN * CAP, 4, 128), F32),
-        vec((2, NBIN, NBIN * CAP, 4, 128), F32),
-        vec((NBIN * NBIN * CAP, 3, 8, 128), F32),
+        vec((3, NBLK, 128), F32),
+        vec((2, NBIN - 1, 3, NBLK, 128), F32),
+        vec((NBIN * (NBLK + 1), 3, 8, 128), F32),
+        vec((NBLK + 1, 2, 4, 8, 128), F32),
+        vec((NBLK + 1, 2, 4, 8, 128), F32),
+        vec((NBLK, 4, 128), F32),
+        vec((NBLK, 4, 128), F32),
+        vec((NBLK, 4, 128), F32),
+        vec((NBLK, 1, 128), F32),
         vec((3, NSEG, 128), F32),
         vec((NSEG, 128), F32),
         vec((NSEG, PIECES * WIDE), F32),
@@ -516,14 +629,19 @@
         vec((16, 128), F32),
         vec((3, 8, 128), F32),
         vec((2, 8, 128), F32),
-        pltpu.SMEM((SUB * NBIN * CAP,), I32),
+        pltpu.SMEM((TABLE,), I32),
+        pltpu.SMEM((NBIN - 1, TABLE), I32),
         dma((5 * ZT,)),
         dma((6,)),
         dma((6,)),
         dma((NBIN - 1,)),
         dma((2, NBIN - 1)),
+        dma((1,)),
+        dma((1,)),
         dma((2,)),
         dma((2,)),
+        dma((NBIN - 1,)),
+        dma((NBIN - 1,)),
     ]
     results = pl.pallas_call(
         kernel,

time: 74.7 us -> 67.2 us (0.90)
  Pallas kernels: 73.4 us -> 65.9 us
    pallas_call x1, Pallas kernels: 72.2 us -> 64.6 us  [per_device(): pl.pallas_call(kernel, out_shape=(pltpu.VMEM((3, CX) + slab, F32), pltpu....]
where the time goes in v4:
time: 67.2 us; the launch traced here: 66.5 us
  Pallas kernels  65.9 us (98%)
    pallas_call x1, Pallas kernels, per_device(): pl.pallas_call(kernel, out_shape=(pltpu.VMEM((3, CX) + slab, F32), pltpu....  64.6 us

profile of v4, /device:TPU:39, one launch (start us, length us, event | category | flops | bytes accessed | tf_op | source)
XLA Modules:
  0.0 66.5 jit_solution(16758111066467803911)
XLA Ops:
  0.6 64.6 %module_substeps.1 = (f32[3,8,4,16,128]{4,3,2,1,0:T(8,128)S(1)}, f32[3,8,4,16,128]{4,3,2,1,0:T(8,128)S(1)}, f32[2,128]{1,0:T(2,128)S(1)}) custom-call(f32[3,8,16,512]{3,2,1,0:T(8,128)} %disp_in.1, f32[3,8,16,512]{3,2,1,0:T(8,128)} %velo_in.1, f32[2,8,16,512]{3,2,1,0:T(8,128)} %moduli_in.1, f32[8,16,512]{2,1,0:T(8,128)} %mass_in.1, s32[8,16,512]{2,1,0:T(8,128)} %tile_in.1, ...), custom_call_target="tpu_custom_call" | custom-call | tf_op jit(solution)/shard_map/module_substeps/pallas_call | solution.py:646
  65.3 1.2 %deliver.1 = (f32[3,8,16,512]{3,2,1,0:T(8,128)}, f32[3,8,16,512]{3,2,1,0:T(8,128)}, f32[2,128]{1,0:T(2,128)}) custom-call(f32[3,8,4,16,128]{4,3,2,1,0:T(8,128)S(1)} %get-tuple-element.9.disp, f32[3,8,4,16,128]{4,3,2,1,0:T(8,128)S(1)} %get-tuple-element.10.velo, f32[2,128]{1,0:T(2,128)S(1)} %get-tuple-element.11.heat), custom_call_target="tpu_custom_call" | custom-call | tf_op jit(solution)/shard_map/deliver/pallas_call | solution.py:664

commit v5 on v4

--- a/solution.py
+++ b/solution.py
@@ -64,13 +64,13 @@
     disp_in, velo_in, moduli_in, mass_in, tile_in, node_ref, base_ref, bins_ref,
     disp_out, velo, heat_out,
     disp, moduli, inverse, tiles,
-    one_seg, one_node, lane_col, base_col, tile_lane, tile_row,
+    one_seg, one_node, lane_col, base_col, tile_lane, tile_row, tile_col,
     split_disp, split_push, seg_col, seg_row, pool, spread,
     met_own, met_over, own_rows, return_out, return_in, heat_row,
     push_acc, heat_acc, picked, pushed,
     grads, stress, near, far,
     col_out, col_in, corner_out, corner_in,
-    layer_force_out, layer_force_in, col_force_out, col_force_in,
+    edge, turned, layer_force_in, col_force_out, col_force_in,
     corner_force_out, corner_force_in,
     heat_parts, heat_in, table, tables,
     in_sem, send_sem, recv_sem, point_send, point_recv, return_send, return_recv,
@@ -105,7 +105,9 @@
         stress[k, 0] = jnp.zeros((ZT, CY, 128), F32)
         stress[k, CX + 1] = jnp.zeros((ZT, CY, 128), F32)
     for p in range(3):
-        far[p, CX, :, 0:8, :] = jnp.zeros((ZT, 8, 128), F32)
+        for k in range(2):
+            for x in range(CX + 1):
+                far[k, p, x, :, 0:8, :] = jnp.zeros((ZT, 8, 128), F32)
         for i in range(NBIN):
             spread[i * (NBLK + 1) + NBLK, p] = jnp.full((8, 128), FAR, F32)
     met_own[NBLK] = jnp.zeros((2, 4, 8, 128), F32)
@@ -183,6 +185,37 @@
 
     lax.fori_loop(0, CX, scale, 0)
 
+    device = dom * bins + own
+
+    def split_tiles(x, carry):
+        offset = tiles[x] - device * TILE_DEV + bins * TILE_DEV
+        side = lax.shift_right_logical(offset, 10)
+        row = side * 2 + (lax.shift_right_logical(offset, 7) & 1)
+        at = pl.ds(pl.multiple_of(x * (ZT * CY), ZT * CY), ZT * CY)
+        split_disp[at, 0:128] = row.astype(F32).astype(BF16).reshape(ZT * CY, 128)
+        lane = (offset & 127).astype(F32).astype(BF16)
+        split_disp[at, 128:256] = lane.reshape(ZT * CY, 128)
+        return carry
+
+    lax.fori_loop(0, CX, split_tiles, 0)
+    picked[:, 0:256] = jnp.dot(
+        one_node[...], split_disp[:, 0:256], preferred_element_type=F32
+    )
+
+    def place_tiles(b, carry):
+        at = pl.ds(pl.multiple_of(b * SEG, SEG), SEG)
+        ids = lanes_of((SEG, SEG)).astype(F32)
+        mask = lane_col[at, :] == ids
+        row_col = jnp.sum(jnp.where(mask, picked[at, 0:128], 0.0), axis=1, keepdims=True)
+        lane = jnp.sum(jnp.where(mask, picked[at, 128:256], 0.0), axis=1, keepdims=True)
+        tile_col[at, :] = jnp.broadcast_to(lane, (SEG, SEG))
+        row = jnp.sum(jnp.where(eye, row_col, 0.0), axis=0, keepdims=True)
+        ids = lax.broadcasted_iota(I32, (16, SEG), 0).astype(F32)
+        tile_row[:, at] = jnp.where(ids == row, 1.0, 0.0).astype(BF16)
+        return carry
+
+    lax.fori_loop(0, NBLK, place_tiles, 0)
+
     greeted = jnp.int32(NBIN - 1)
     for _, _, exists in peers[NBIN - 1 :]:
         greeted = greeted + exists.astype(I32)
@@ -207,7 +240,7 @@
     layer_copy = remote(disp.at[:, 0, :, inner, :], disp.at[:, CX, :, inner, :], 0, dom - 1, own)
     col_copy = remote(col_out, col_in, 1, dom, own - 1)
     corner_copy = remote(corner_out, corner_in, 2, dom - 1, own - 1)
-    layer_force_copy = remote(layer_force_out, layer_force_in, 3, dom + 1, own)
+    layer_force_copy = remote(near.at[:, CX], layer_force_in, 3, dom + 1, own)
     col_force_copy = remote(col_force_out, col_force_in, 4, dom, own + 1)
     corner_force_copy = remote(corner_force_out, corner_force_in, 5, dom + 1, own + 1)
 
@@ -277,6 +310,34 @@
     def rows_of(values):
         return jnp.sum(functools.reduce(lambda a, b: a + b, values), axis=0, keepdims=True)
 
+    def heat_copy(index, to_dom):
+        return pltpu.make_async_remote_copy(
+            src_ref=heat_parts.at[2 * index], dst_ref=heat_in.at[index],
+            send_sem=heat_send.at[index], recv_sem=heat_recv.at[index],
+            device_id=(to_dom, own), device_id_type=MESH,
+        )
+
+    to_low, to_up = heat_copy(0, dom - 1), heat_copy(1, dom + 1)
+
+    def send_heat():
+        def lay_heat(b, carry):
+            at = pl.ds(pl.multiple_of(b * SEG, SEG), SEG)
+            met = heat_row[b] + own_rows[b, 3:4, :] + return_in[b, 3:4, :]
+            total = heat_acc[at, :] + jnp.where(eye, met, 0.0)
+            total = SHORT_GAIN * jnp.sum(total, axis=1, keepdims=True)
+            laid = jnp.where(tile_col[at, :] == lanes_of((SEG, SEG)).astype(F32), total, 0.0)
+            for p, part in enumerate(pieces_of(laid)):
+                tile_lane[at, p * 128 : p * 128 + 128] = part
+            return carry
+
+        lax.fori_loop(0, NBLK, lay_heat, 0)
+        laid = jnp.dot(tile_row[...], tile_lane[...], preferred_element_type=F32)
+        on_tiles = laid[:, 0:128] + laid[:, 128:256]
+        for side in range(3):
+            heat_parts[side, 0:2, :] = on_tiles[side * 2 : side * 2 + 2, :]
+        pl.when(dom_low)(to_low.start)
+        pl.when(dom_up)(to_up.start)
+
     def substep(step, carry):
         parity = lax.rem(step, 2)
 
@@ -343,16 +404,23 @@
                 disp[c, CX, z, 24:25, :] = corner_in[c * ZT + z : c * ZT + z + 1, :]
                 for x in range(CX):
                     disp[c, x, z, 24:25, :] = col_in[c, z, x : x + 1, :]
+            edge[...] = next_z(col_in[c])
+            for z in range(ZT):
+                for x in range(CX):
+                    turned[c, x, z, 24:25, :] = edge[z, x : x + 1, :]
+            turned[c, CX, :, 24:32, :] = next_z(disp[c, CX, :, 24:32, :])
 
         def corners(part, carry):
             for x in [3 * part + i for i in range(3)]:
                 for c in range(3):
                     low, high = disp[c, x, :, 8:24, :], disp[c, x, :, 9:25, :]
-                    total, gap = low + high, high - low
-                    total_next, gap_next = next_z(total), next_z(gap)
-                    grads[c, 0, x] = total + total_next
-                    grads[c, 1, x] = gap + gap_next
-                    grads[c, 2, x] = total_next - total
+                    low_next = next_z(low)
+                    turned[c, x, :, 8:24, :] = low_next
+                    high_next = turned[c, x, :, 9:25, :]
+                    at_low, at_high = low + low_next, high + high_next
+                    grads[c, 0, x] = at_low + at_high
+                    grads[c, 1, x] = at_high - at_low
+                    grads[c, 2, x] = (low_next - low) + (high_next - high)
             return carry
 
         lax.fori_loop(0, (CX + 1) // 3, corners, 0)
@@ -380,14 +448,16 @@
                 along_y = stress[ky, x] + stress[ky, x + 1]
                 along_z = stress[kz, x] + stress[kz, x + 1]
                 minus, plus = along_x - along_y, along_x + along_y
-                near[p, x] = (minus - along_z) + last_z(minus + along_z)
-                far[p, x, :, 8:24, :] = (plus - along_z) + last_z(plus + along_z)
+                far[0, p, x, :, 8:24, :] = plus - along_z
+                far[1, p, x, :, 8:24, :] = plus + along_z
+                here = minus - along_z + far[0, p, x, :, 7:23, :]
+                near[p, x] = here + last_z(minus + along_z + far[1, p, x, :, 7:23, :])
 
         forces_on(CX)
         for p in range(3):
-            layer_force_out[p] = near[p, CX] + far[p, CX, :, 7:23, :]
+            ends = far[0, p, CX, :, 16:24, :] + last_z(far[1, p, CX, :, 16:24, :])
             for z in range(ZT):
-                corner_force_out[p * ZT + z : p * ZT + z + 1, :] = far[p, CX, z, 23:24, :]
+                corner_force_out[p * ZT + z : p * ZT + z + 1, :] = ends[z, 7:8, :]
         pl.when(dom_up)(layer_force_copy.start)
         pl.when(diag_up)(corner_force_copy.start)
 
@@ -400,7 +470,9 @@
         for p in range(3):
             for z in range(ZT):
                 for x in range(CX):
-                    col_force_out[p, z, x : x + 1, :] = far[p, x, z, 23:24, :]
+                    col_force_out[p, z, x : x + 1, :] = far[0, p, x, z, 23:24, :]
+                    edge[z, x : x + 1, :] = far[1, p, x, z, 23:24, :]
+            col_force_out[p] = col_force_out[p] + last_z(edge[...])
         pl.when(bin_up)(col_force_copy.start)
 
         @pl.when(step == 0)
@@ -436,6 +508,8 @@
         touching(step, next_slots, None, ROWS_NEXT, 2 * CAP)
 
         return_copy.wait_recv()
+        pl.when(step == SUB - 1)(send_heat)
+
 
         def lay_push(pair, carry):
             for b in (2 * pair, 2 * pair + 1):
@@ -464,7 +538,9 @@
                     near[p, 0, z, 0:1, :] + corner_force_in[p * ZT + z : p * ZT + z + 1, :]
                 )
                 for x in range(CX):
-                    far[p, x, z, 7:8, :] = col_force_in[p, z, x : x + 1, :]
+                    near[p, x, z, 0:1, :] = (
+                        near[p, x, z, 0:1, :] + col_force_in[p, z, x : x + 1, :]
+                    )
         pl.when(dom_low)(layer_copy.wait_send)
         pl.when(bin_low)(col_copy.wait_send)
         pl.when(diag_low)(corner_copy.wait_send)
@@ -478,7 +554,7 @@
         def advance(x, carry):
             for p in range(3):
                 at = pl.ds(pl.multiple_of(x * (ZT * CY), ZT * CY), ZT * CY)
-                force = near[p, x] + far[p, x, :, 7:23, :]
+                force = near[p, x]
                 for part in range(PIECES):
                     column = part * WIDE + p * 128
                     force = force + pushed[at, column : column + 128].reshape(ZT, CY, 128)
@@ -506,59 +582,6 @@
 
     lax.fori_loop(0, SUB, substep, 0)
 
-    device = dom * bins + own
-
-    def split_tiles(x, carry):
-        offset = tiles[x] - device * TILE_DEV + bins * TILE_DEV
-        side = lax.shift_right_logical(offset, 10)
-        row = side * 2 + (lax.shift_right_logical(offset, 7) & 1)
-        at = pl.ds(pl.multiple_of(x * (ZT * CY), ZT * CY), ZT * CY)
-        split_disp[at, 0:128] = row.astype(F32).astype(BF16).reshape(ZT * CY, 128)
-        lane = (offset & 127).astype(F32).astype(BF16)
-        split_disp[at, 128:256] = lane.reshape(ZT * CY, 128)
-        return carry
-
-    lax.fori_loop(0, CX, split_tiles, 0)
-
-    def lay_heat(b, carry):
-        at = pl.ds(pl.multiple_of(b * SEG, SEG), SEG)
-        picked = jnp.dot(
-            one_node[at, :], split_disp[:, 0:256], preferred_element_type=F32
-        )
-        ids = lanes_of((SEG, SEG)).astype(F32)
-        mask = lane_col[at, :] == ids
-        row_col = jnp.sum(jnp.where(mask, picked[:, 0:128], 0.0), axis=1, keepdims=True)
-        lane = jnp.sum(jnp.where(mask, picked[:, 128:256], 0.0), axis=1, keepdims=True)
-        tile_row[b, 0:1, :] = jnp.sum(jnp.where(eye, row_col, 0.0), axis=0, keepdims=True)
-        total = heat_acc[at, :] + jnp.where(eye, heat_row[b], 0.0)
-        total = SHORT_GAIN * jnp.sum(total, axis=1, keepdims=True)
-        laid = jnp.where(lane == ids, total, 0.0)
-        for p, part in enumerate(pieces_of(laid)):
-            tile_lane[p, at, :] = part
-        return carry
-
-    lax.fori_loop(0, NBLK, lay_heat, 0)
-    on_tiles = jnp.zeros((16, 128), F32)
-    for b in range(NBLK):
-        ids = lax.broadcasted_iota(I32, (16, SEG), 0).astype(F32)
-        hits = jnp.where(ids == tile_row[b, 0:1, :], 1.0, 0.0).astype(BF16)
-        for p in range(PIECES):
-            on_tiles = on_tiles + jnp.dot(
-                hits, tile_lane[p, b * SEG : (b + 1) * SEG, :], preferred_element_type=F32
-            )
-    for side in range(3):
-        heat_parts[side, 0:2, :] = on_tiles[side * 2 : side * 2 + 2, :]
-
-    def heat_copy(index, to_dom):
-        return pltpu.make_async_remote_copy(
-            src_ref=heat_parts.at[2 * index], dst_ref=heat_in.at[index],
-            send_sem=heat_send.at[index], recv_sem=heat_recv.at[index],
-            device_id=(to_dom, own), device_id_type=MESH,
-        )
-
-    to_low, to_up = heat_copy(0, dom - 1), heat_copy(1, dom + 1)
-    pl.when(dom_low)(to_low.start)
-    pl.when(dom_up)(to_up.start)
     pl.when(dom_up)(to_low.wait_recv)
     pl.when(dom_low)(to_up.wait_recv)
     heat_out[...] = heat_parts[1, 0:2, :] + heat_in[0, 0:2, :] + heat_in[1, 0:2, :]
@@ -595,8 +618,9 @@
         vec((NSEG, ROWS), BF16),
         vec((NSEG, 128), F32),
         vec((3, NSEG, 128), F32),
-        vec((PIECES, NSEG, 128), BF16),
-        vec((NBLK, 8, 128), F32),
+        vec((NSEG, PIECES * 128), BF16),
+        vec((16, NSEG), BF16),
+        vec((NSEG, 128), F32),
         vec((ROWS, PIECES * WIDE), BF16),
         vec((NSEG, PIECES * WIDE), BF16),
         vec((3, NSEG, 128), F32),
@@ -616,12 +640,13 @@
         vec((3, 3, CX + 1) + slab, F32),
         vec((6, CX + 2) + slab, F32),
         vec((3, CX + 1) + slab, F32),
-        vec((3, CX + 1, ZT, 32, 128), F32),
+        vec((2, 3, CX + 1, ZT, 32, 128), F32),
         vec((3, ZT, CX, 128), F32),
         vec((3, ZT, CX, 128), F32),
         vec((16, 128), F32),
         vec((16, 128), F32),
-        vec((3,) + slab, F32),
+        vec((ZT, CX, 128), F32),
+        vec((3, CX + 1, ZT, 32, 128), F32),
         vec((3,) + slab, F32),
         vec((3, ZT, CX, 128), F32),
         vec((3, ZT, CX, 128), F32),

time: 67.2 us -> 64.1 us (0.954)
  Pallas kernels: 65.9 us -> 62.3 us
    pallas_call x1, Pallas kernels: 64.6 us -> 61.1 us  [per_device(): pl.pallas_call(kernel, out_shape=(pltpu.VMEM((3, CX) + slab, F32), pltpu....]
where the time goes in v5:
time: 64.1 us; the launch traced here: 63 us
  Pallas kernels  62.3 us (97%)
    pallas_call x1, Pallas kernels, per_device(): pl.pallas_call(kernel, out_shape=(pltpu.VMEM((3, CX) + slab, F32), pltpu....  61.1 us

profile of v5, /device:TPU:39, one launch (start us, length us, event | category | flops | bytes accessed | tf_op | source)
XLA Modules:
  0.0 63.0 jit_solution(16854220740050999725)
XLA Ops:
  0.6 61.1 %module_substeps.1 = (f32[3,8,4,16,128]{4,3,2,1,0:T(8,128)S(1)}, f32[3,8,4,16,128]{4,3,2,1,0:T(8,128)S(1)}, f32[2,128]{1,0:T(2,128)S(1)}) custom-call(f32[3,8,16,512]{3,2,1,0:T(8,128)} %disp_in.1, f32[3,8,16,512]{3,2,1,0:T(8,128)} %velo_in.1, f32[2,8,16,512]{3,2,1,0:T(8,128)} %moduli_in.1, f32[8,16,512]{2,1,0:T(8,128)} %mass_in.1, s32[8,16,512]{2,1,0:T(8,128)} %tile_in.1, ...), custom_call_target="tpu_custom_call" | custom-call | tf_op jit(solution)/shard_map/module_substeps/pallas_call | solution.py:671
  61.8 1.2 %deliver.1 = (f32[3,8,16,512]{3,2,1,0:T(8,128)}, f32[3,8,16,512]{3,2,1,0:T(8,128)}, f32[2,128]{1,0:T(2,128)}) custom-call(f32[3,8,4,16,128]{4,3,2,1,0:T(8,128)S(1)} %get-tuple-element.9.disp, f32[3,8,4,16,128]{4,3,2,1,0:T(8,128)S(1)} %get-tuple-element.10.velo, f32[2,128]{1,0:T(2,128)S(1)} %get-tuple-element.11.heat), custom_call_target="tpu_custom_call" | custom-call | tf_op jit(solution)/shard_map/deliver/pallas_call | solution.py:689

commit v6 on v5

--- a/solution.py
+++ b/solution.py
@@ -152,7 +152,7 @@
 
     eye = lax.broadcasted_iota(I32, (SEG, SEG), 0) == lanes_of((SEG, SEG))
 
-    def place_block(b, carry):
+    def place_block(b):
         node = node_ref[pl.ds(b, 1), :]
         x, y = lax.shift_right_logical(node, 13), lax.shift_right_logical(node, 9) & 15
         z = lax.shift_right_logical(node, 7) & 3
@@ -170,9 +170,13 @@
         for c in range(3):
             base_col[c, at, :] = spread_row(base_ref[c : c + 1, at])
         heat_acc[at, :] = jnp.zeros((SEG, SEG), F32)
+
+    def place_pair(pair, carry):
+        for b in (2 * pair, 2 * pair + 1):
+            place_block(b)
         return carry
 
-    lax.fori_loop(0, NBLK, place_block, 0)
+    lax.fori_loop(0, NBLK // 2, place_pair, 0)
 
     for load in loads:
         load.wait()
@@ -184,37 +188,6 @@
         return carry
 
     lax.fori_loop(0, CX, scale, 0)
-
-    device = dom * bins + own
-
-    def split_tiles(x, carry):
-        offset = tiles[x] - device * TILE_DEV + bins * TILE_DEV
-        side = lax.shift_right_logical(offset, 10)
-        row = side * 2 + (lax.shift_right_logical(offset, 7) & 1)
-        at = pl.ds(pl.multiple_of(x * (ZT * CY), ZT * CY), ZT * CY)
-        split_disp[at, 0:128] = row.astype(F32).astype(BF16).reshape(ZT * CY, 128)
-        lane = (offset & 127).astype(F32).astype(BF16)
-        split_disp[at, 128:256] = lane.reshape(ZT * CY, 128)
-        return carry
-
-    lax.fori_loop(0, CX, split_tiles, 0)
-    picked[:, 0:256] = jnp.dot(
-        one_node[...], split_disp[:, 0:256], preferred_element_type=F32
-    )
-
-    def place_tiles(b, carry):
-        at = pl.ds(pl.multiple_of(b * SEG, SEG), SEG)
-        ids = lanes_of((SEG, SEG)).astype(F32)
-        mask = lane_col[at, :] == ids
-        row_col = jnp.sum(jnp.where(mask, picked[at, 0:128], 0.0), axis=1, keepdims=True)
-        lane = jnp.sum(jnp.where(mask, picked[at, 128:256], 0.0), axis=1, keepdims=True)
-        tile_col[at, :] = jnp.broadcast_to(lane, (SEG, SEG))
-        row = jnp.sum(jnp.where(eye, row_col, 0.0), axis=0, keepdims=True)
-        ids = lax.broadcasted_iota(I32, (16, SEG), 0).astype(F32)
-        tile_row[:, at] = jnp.where(ids == row, 1.0, 0.0).astype(BF16)
-        return carry
-
-    lax.fori_loop(0, NBLK, place_tiles, 0)
 
     greeted = jnp.int32(NBIN - 1)
     for _, _, exists in peers[NBIN - 1 :]:
@@ -310,6 +283,38 @@
     def rows_of(values):
         return jnp.sum(functools.reduce(lambda a, b: a + b, values), axis=0, keepdims=True)
 
+    device = dom * bins + own
+
+    def find_tiles():
+
+        def split_tiles(x, carry):
+            offset = tiles[x] - device * TILE_DEV + bins * TILE_DEV
+            side = lax.shift_right_logical(offset, 10)
+            row = side * 2 + (lax.shift_right_logical(offset, 7) & 1)
+            at = pl.ds(pl.multiple_of(x * (ZT * CY), ZT * CY), ZT * CY)
+            split_disp[0, at, :] = row.astype(F32).astype(BF16).reshape(ZT * CY, 128)
+            lane = (offset & 127).astype(F32).astype(BF16)
+            split_disp[1, at, :] = lane.reshape(ZT * CY, 128)
+            return carry
+
+        lax.fori_loop(0, CX, split_tiles, 0)
+        side_by_side = jnp.concatenate([split_disp[0], split_disp[1]], axis=1)
+        picked[:, 0:256] = jnp.dot(one_node[...], side_by_side, preferred_element_type=F32)
+
+        def place_tiles(b, carry):
+            at = pl.ds(pl.multiple_of(b * SEG, SEG), SEG)
+            ids = lanes_of((SEG, SEG)).astype(F32)
+            mask = lane_col[at, :] == ids
+            row_col = jnp.sum(jnp.where(mask, picked[at, 0:128], 0.0), axis=1, keepdims=True)
+            lane = jnp.sum(jnp.where(mask, picked[at, 128:256], 0.0), axis=1, keepdims=True)
+            tile_col[at, :] = jnp.broadcast_to(lane, (SEG, SEG))
+            row = jnp.sum(jnp.where(eye, row_col, 0.0), axis=0, keepdims=True)
+            ids = lax.broadcasted_iota(I32, (16, SEG), 0).astype(F32)
+            tile_row[:, at] = jnp.where(ids == row, 1.0, 0.0).astype(BF16)
+            return carry
+
+        lax.fori_loop(0, NBLK, place_tiles, 0)
+
     def heat_copy(index, to_dom):
         return pltpu.make_async_remote_copy(
             src_ref=heat_parts.at[2 * index], dst_ref=heat_in.at[index],
@@ -346,7 +351,6 @@
                 corner_out[c * ZT + z : c * ZT + z + 1, :] = disp[c, 0, z, 8:9, :]
                 for x in range(CX):
                     col_out[c, z, x : x + 1, :] = disp[c, x, z, 8:9, :]
-        pl.when(dom_low)(layer_copy.start)
         pl.when(bin_low)(col_copy.start)
         pl.when(diag_low)(corner_copy.start)
 
@@ -356,21 +360,24 @@
                 for c in range(3):
                     value = disp[c, x, :, 8 : 8 + CY, :].reshape(ZT * CY, 128)
                     for p, part in enumerate(pieces_of(value)):
-                        split_disp[at, p * WIDE + c * 128 : p * WIDE + c * 128 + 128] = part
+                        split_disp[p * 3 + c, at, :] = part
             return carry
 
         lax.fori_loop(0, CX // 2, split, 0)
-        picked[...] = jnp.dot(one_node[...], split_disp[...], preferred_element_type=F32)
+        side_by_side = jnp.concatenate([split_disp[k] for k in range(PIECES * 3)], axis=1)
+        picked[...] = jnp.dot(one_node[...], side_by_side, preferred_element_type=F32)
 
         def positions(pair, carry):
             for b in (2 * pair, 2 * pair + 1):
                 at = pl.ds(pl.multiple_of(b * SEG, SEG), SEG)
                 mask = lane_col[at, :] == lanes_of((SEG, SEG)).astype(F32)
                 for c in range(3):
-                    value = picked[at, c * 128 : c * 128 + 128]
-                    value = value + picked[at, WIDE + c * 128 : WIDE + c * 128 + 128]
-                    moved = jnp.where(mask, value, 0.0)
-                    column = base_col[c, at, :] + jnp.sum(moved, axis=1, keepdims=True)
+                    parts = [
+                        jnp.where(mask, picked[at, k : k + 128], 0.0)
+                        for k in range(c * 128, PIECES * WIDE, WIDE)
+                    ]
+                    total = jnp.sum(parts[0] + parts[1], axis=1, keepdims=True)
+                    column = base_col[c, at, :] + total
                     seg_col[c, at, :] = column
                     row = jnp.sum(jnp.where(eye, column, 0.0), axis=0, keepdims=True)
                     seg_row[c, pl.ds(b, 1), :] = row
@@ -378,7 +385,7 @@
             return carry
 
         lax.fori_loop(0, NBLK // 2, positions, 0)
-        for i in range(NBIN - 1):
+        for i in (1, 0, 2):
             point_copy(i, parity).start()
 
         touching(step, own_slots, met_own, ROWS_OWN, 1)
@@ -396,36 +403,35 @@
 
         lax.fori_loop(0, NBLK, gather_own, 0)
 
-        pl.when(dom_up)(layer_copy.wait_recv)
         pl.when(bin_up)(col_copy.wait_recv)
-        pl.when(diag_up)(corner_copy.wait_recv)
         for c in range(3):
             for z in range(ZT):
-                disp[c, CX, z, 24:25, :] = corner_in[c * ZT + z : c * ZT + z + 1, :]
                 for x in range(CX):
                     disp[c, x, z, 24:25, :] = col_in[c, z, x : x + 1, :]
             edge[...] = next_z(col_in[c])
             for z in range(ZT):
                 for x in range(CX):
                     turned[c, x, z, 24:25, :] = edge[z, x : x + 1, :]
-            turned[c, CX, :, 24:32, :] = next_z(disp[c, CX, :, 24:32, :])
+
+        def corners_on(x):
+            for c in range(3):
+                low, high = disp[c, x, :, 8:24, :], disp[c, x, :, 9:25, :]
+                low_next = next_z(low)
+                turned[c, x, :, 8:24, :] = low_next
+                high_next = turned[c, x, :, 9:25, :]
+                at_low, at_high = low + low_next, high + high_next
+                grads[c, 0, x] = at_low + at_high
+                grads[c, 1, x] = at_high - at_low
+                grads[c, 2, x] = (low_next - low) + (high_next - high)
 
         def corners(part, carry):
-            for x in [3 * part + i for i in range(3)]:
-                for c in range(3):
-                    low, high = disp[c, x, :, 8:24, :], disp[c, x, :, 9:25, :]
-                    low_next = next_z(low)
-                    turned[c, x, :, 8:24, :] = low_next
-                    high_next = turned[c, x, :, 9:25, :]
-                    at_low, at_high = low + low_next, high + high_next
-                    grads[c, 0, x] = at_low + at_high
-                    grads[c, 1, x] = at_high - at_low
-                    grads[c, 2, x] = (low_next - low) + (high_next - high)
-            return carry
-
-        lax.fori_loop(0, (CX + 1) // 3, corners, 0)
-
-        def stresses(x, carry):
+            for x in [4 * part + i for i in range(4)]:
+                corners_on(x)
+            return carry
+
+        lax.fori_loop(0, CX // 4, corners, 0)
+
+        def stresses_on(x):
             g = [
                 [grads[c, 0, x + 1] - grads[c, 0, x]]
                 + [grads[c, q, x] + grads[c, q, x + 1] for q in (1, 2)]
@@ -438,9 +444,20 @@
             stress[3, x + 1] = shear * (g[0][1] + g[1][0])
             stress[4, x + 1] = shear * (g[0][2] + g[2][0])
             stress[5, x + 1] = shear * (g[1][2] + g[2][1])
-            return carry
-
-        lax.fori_loop(0, CX, stresses, 0)
+
+        def stresses(x, carry):
+            stresses_on(x)
+            return carry
+
+        lax.fori_loop(0, CX - 1, stresses, 0)
+        pl.when(dom_up)(layer_copy.wait_recv)
+        pl.when(diag_up)(corner_copy.wait_recv)
+        for c in range(3):
+            for z in range(ZT):
+                disp[c, CX, z, 24:25, :] = corner_in[c * ZT + z : c * ZT + z + 1, :]
+            turned[c, CX, :, 24:32, :] = next_z(disp[c, CX, :, 24:32, :])
+        corners_on(CX)
+        stresses_on(CX - 1)
 
         def forces_on(x):
             for p, (kx, ky, kz) in enumerate(((0, 3, 4), (3, 1, 5), (4, 5, 2))):
@@ -474,6 +491,8 @@
                     edge[z, x : x + 1, :] = far[1, p, x, z, 23:24, :]
             col_force_out[p] = col_force_out[p] + last_z(edge[...])
         pl.when(bin_up)(col_force_copy.start)
+
+        pl.when(step == 1)(find_tiles)
 
         @pl.when(step == 0)
         def tables_here():
@@ -522,11 +541,12 @@
                     total = jnp.sum(total, axis=1, keepdims=True)
                     laid = jnp.where(mask, PENALTY * total, 0.0)
                     for p, part in enumerate(pieces_of(laid)):
-                        split_push[at, p * WIDE + c * 128 : p * WIDE + c * 128 + 128] = part
+                        split_push[p * 3 + c, at, :] = part
             return carry
 
         lax.fori_loop(0, NBLK // 2, lay_push, 0)
-        pushed[...] = jnp.dot(one_seg[...], split_push[...], preferred_element_type=F32)
+        side_by_side = jnp.concatenate([split_push[k] for k in range(PIECES * 3)], axis=1)
+        pushed[...] = jnp.dot(one_seg[...], side_by_side, preferred_element_type=F32)
 
         pl.when(dom_low)(layer_force_copy.wait_recv)
         pl.when(bin_low)(col_force_copy.wait_recv)
@@ -551,9 +571,9 @@
             point_copy(i, parity).wait_send()
         return_copy.wait_send()
 
-        def advance(x, carry):
+        def advance_on(x):
+            at = pl.ds(x * (ZT * CY), ZT * CY)
             for p in range(3):
-                at = pl.ds(pl.multiple_of(x * (ZT * CY), ZT * CY), ZT * CY)
                 force = near[p, x]
                 for part in range(PIECES):
                     column = part * WIDE + p * 128
@@ -563,9 +583,14 @@
                 moved = disp[p, x, :, 8:24, :] + TIME_STEP * moved
                 disp[p, x, :, 8:24, :] = moved
                 disp_out[p, x] = moved
-            return carry
-
-        lax.fori_loop(0, CX, advance, 0)
+
+        def advance(x, carry):
+            advance_on(pl.multiple_of(x, 1))
+            return carry
+
+        advance_on(0)
+        pl.when(jnp.logical_and(dom_low, step < SUB - 1))(layer_copy.start)
+        lax.fori_loop(1, CX, advance, 0)
         return carry
 
     def point_copy(i, parity):
@@ -580,6 +605,7 @@
         recv_sem=return_recv.at[0], device_id=(dom, lax.rem(own + 2, bins)), device_id_type=MESH,
     )
 
+    pl.when(dom_low)(layer_copy.start)
     lax.fori_loop(0, SUB, substep, 0)
 
     pl.when(dom_up)(to_low.wait_recv)
@@ -621,8 +647,8 @@
         vec((NSEG, PIECES * 128), BF16),
         vec((16, NSEG), BF16),
         vec((NSEG, 128), F32),
-        vec((ROWS, PIECES * WIDE), BF16),
-        vec((NSEG, PIECES * WIDE), BF16),
+        vec((PIECES * 3, ROWS, 128), BF16),
+        vec((PIECES * 3, NSEG, 128), BF16),
         vec((3, NSEG, 128), F32),
         vec((3, NBLK, 128), F32),
         vec((2, NBIN - 1, 3, NBLK, 128), F32),

time: 64.1 us -> 62.6 us (0.977)
  Pallas kernels: 62.3 us -> 61.3 us
    pallas_call x1, Pallas kernels: 61.1 us -> 60.1 us  [per_device(): pl.pallas_call(kernel, out_shape=(pltpu.VMEM((3, CX) + slab, F32), pltpu....]
where the time goes in v6:
time: 62.6 us; the launch traced here: 61.9 us
  Pallas kernels  61.3 us (98%)
  between operations  0.64 us (1%)
    pallas_call x1, Pallas kernels, per_device(): pl.pallas_call(kernel, out_shape=(pltpu.VMEM((3, CX) + slab, F32), pltpu....  60.1 us

profile of v6, /device:TPU:39, one launch (start us, length us, event | category | flops | bytes accessed | tf_op | source)
XLA Modules:
  0.0 61.9 jit_solution(9984678409568022121)
XLA Ops:
  0.6 60.1 %module_substeps.1 = (f32[3,8,4,16,128]{4,3,2,1,0:T(8,128)S(1)}, f32[3,8,4,16,128]{4,3,2,1,0:T(8,128)S(1)}, f32[2,128]{1,0:T(2,128)S(1)}) custom-call(f32[3,8,16,512]{3,2,1,0:T(8,128)} %disp_in.1, f32[3,8,16,512]{3,2,1,0:T(8,128)} %velo_in.1, f32[2,8,16,512]{3,2,1,0:T(8,128)} %moduli_in.1, f32[8,16,512]{2,1,0:T(8,128)} %mass_in.1, s32[8,16,512]{2,1,0:T(8,128)} %tile_in.1, ...), custom_call_target="tpu_custom_call" | custom-call | tf_op jit(solution)/shard_map/module_substeps/pallas_call | solution.py:697
  60.7 1.2 %deliver.1 = (f32[3,8,16,512]{3,2,1,0:T(8,128)}, f32[3,8,16,512]{3,2,1,0:T(8,128)}, f32[2,128]{1,0:T(2,128)}) custom-call(f32[3,8,4,16,128]{4,3,2,1,0:T(8,128)S(1)} %get-tuple-element.9.disp, f32[3,8,4,16,128]{4,3,2,1,0:T(8,128)S(1)} %get-tuple-element.10.velo, f32[2,128]{1,0:T(2,128)S(1)} %get-tuple-element.11.heat), custom_call_target="tpu_custom_call" | custom-call | tf_op jit(solution)/shard_map/deliver/pallas_call | solution.py:715
